TPU v7x, 512 devices: a whole 4x4x16 slice. The times are simulated.
512 devices in a mesh: gx: 128 (over z, y, core), gy: 4 (over x).
Axes of the slice: x: 4, y: 4, z: 16, core: 2. Of those that a mesh axis runs over, the one named last changes fastest.
Arguments:
- right_side: float32 [12, 2048, 8192], P(None, 'gx', 'gy'), may hold values from -6 to 6
- diffusion: float32 [2048, 8192], P('gx', 'gy'), may hold values from 0.5 to 2
- drift_field: float32 [2, 2048, 8192], P(None, 'gx', 'gy'), may hold values from -3 to 3
- shifts: float32 [6, 2], replicated, may hold values from 1 to 4
Outputs:
- solution: float32 [12, 2048, 8192], P(None, 'gx', 'gy')
All inputs are finite; a program needn't handle non-finite values.
Results may differ from a plain program's by a relative error of at most 0.00027.
Values sent between devices are 32-bit elements; how exact they have to be, the bound alone decides.
No kernel may reach another device: no remote copies, remote signals or barrier semaphores. Data moves between devices by JAX's collectives and lax.ppermute only.
A program may use at most 64 MiB of HBM per device.

v0:
```python
import jax
import jax.numpy as jnp
import numpy as np
from jax import lax
from jax.sharding import PartitionSpec as P

S = 4


newton_shifts = (-8.0, -2.0, -14.0, -5.0)
newton_scale = 8.0
highest = lax.Precision.HIGHEST


def padded_2(block, sides, width, periodic):
    for axis, dim in sides:
        count = lax.axis_size(axis)
        forward = [(i, i + 1) for i in range(count - 1)]
        if periodic:
            forward.append((count - 1, 0))
        backward = [(target, source) for source, target in forward]
        low = lax.ppermute(
            lax.slice_in_dim(block, block.shape[dim] - width, None, axis=dim), axis, forward
        )
        high = lax.ppermute(lax.slice_in_dim(block, 0, width, axis=dim), axis, backward)
        block = jnp.concatenate([low, block, high], axis=dim)
    return block


def generator(padded, diffusion, drift_field):
    center = padded[:, 1:-1, 1:-1]
    forward_x = padded[:, 2:, 1:-1]
    backward_x = padded[:, :-2, 1:-1]
    forward_y = padded[:, 1:-1, 2:]
    backward_y = padded[:, 1:-1, :-2]
    spread_term = diffusion * (forward_x + backward_x + forward_y + backward_y - 4.0 * center)
    return (
        spread_term
        + 0.5 * drift_field[0] * (forward_x - backward_x)
        + 0.5 * drift_field[1] * (forward_y - backward_y)
    )


def newton_step(padded, diffusion, drift_field, degree):
    center = padded[:, 1:-1, 1:-1]
    return (
        generator(padded, diffusion, drift_field) - newton_shifts[degree] * center
    ) / newton_scale


def change_matrix(channels, degrees):
    change_table = np.zeros(((degrees + 1) * channels, degrees * channels), np.float32)
    for degree in range(degrees):
        for component in range(channels):
            column = degree * channels + component
            change_table[column, column] = newton_shifts[degree]
            change_table[column + channels, column] = newton_scale
    return change_table


def solve_shifts(upper_factor, shifts):
    channels = 2 * shifts.shape[0]
    columns = upper_factor.shape[1] - channels
    change = jnp.asarray(change_matrix(channels, columns // channels))
    select = jnp.asarray(np.eye(upper_factor.shape[0], columns, dtype=np.float32))

    def single(shift_index):
        shift_real = shifts[shift_index, 0]
        shift_imag = shifts[shift_index, 1]
        real_part = jnp.dot(upper_factor, change - shift_real * select, precision=highest)
        imag_part = -shift_imag * upper_factor[:, :columns]
        system = jnp.concatenate(
            [
                jnp.concatenate([real_part, -imag_part], axis=1),
                jnp.concatenate([imag_part, real_part], axis=1),
            ],
            axis=0,
        )
        target = jnp.concatenate(
            [upper_factor[:, 2 * shift_index], upper_factor[:, 2 * shift_index + 1]]
        )
        normal = jnp.dot(system.T, system, precision=highest)
        moment = jnp.dot(system.T, target, precision=highest)[:, None]
        factor = jnp.linalg.cholesky(normal)
        middle = lax.linalg.triangular_solve(factor, moment, left_side=True, lower=True)
        answer = lax.linalg.triangular_solve(
            factor, middle, left_side=True, lower=True, transpose_a=True
        )
        answer = answer[:, 0]
        return (answer[:columns], answer[columns:])

    real_parts, imag_parts = jax.vmap(single)(jnp.arange(shifts.shape[0]))
    return jnp.stack([real_parts, imag_parts], axis=1).reshape(channels, columns)


def per_device(right_side, diffusion, drift_field, shifts):
    channels = right_side.shape[0]
    tile_rows = right_side.shape[1]
    tile_cols = right_side.shape[2]
    krylov = [right_side]
    current = right_side
    for degree in range(S):
        widened = padded_2(current, (("gx", 1),), 1, True)
        padded = padded_2(widened, (("gy", 2),), 1, False)
        current = newton_step(padded, diffusion, drift_field, degree)
        krylov.append(current)
    basis_rows = jnp.stack(krylov).reshape(len(krylov) * channels, tile_rows * tile_cols)
    local_gram = jnp.dot(basis_rows, basis_rows.T, precision=highest)
    global_gram = lax.psum(local_gram, ("gx", "gy"))
    upper_factor = jnp.linalg.cholesky(global_gram).T
    mixing = solve_shifts(upper_factor, shifts)
    columns = mixing.shape[1]
    solution = jnp.dot(mixing, basis_rows[:columns], precision=highest)
    return solution.reshape(channels, tile_rows, tile_cols)


def solution(mesh):
    in_specs = (P(None, "gx", "gy"), P("gx", "gy"), P(None, "gx", "gy"), P())
    out_specs = P(None, "gx", "gy")
    return jax.shard_map(
        per_device, mesh=mesh, in_specs=in_specs, out_specs=out_specs, check_vma=False
    )
```

profile of v0, /device:TPU:1, one launch (start us, length us, event | category | flops | bytes accessed | tf_op | source)
XLA Modules:
  0.0 347.6 jit_solution(17700932143488236161)
XLA Ops:
  0.0 1.5 fusion.34
  1.5 8.7 %collective-permute-start = (f32[12,1,2048]{2,1,0:T(1,128)S(1)}, f32[12,1,2048]{2,1,0:T(1,128)S(1)}, u32[]{:S(2)}, u32[]{:S(2)}) collective-permute-start(f32[12,1,2048]{2,1,0:T(1,128)S(1)} %get-tuple-element.26), channel_id=1, source_target_pairs={{4,0},{8,4},{12,8},{16,12},{20,16},{24,20},{28,24},{32,28},{36,32}... | collective-permute-start | bytes 294920 | tf_op jit(solution)/shard_map/ppermute | solution.py:25
  10.3 2.1 collective-permute-start.1
  12.4 2.7 constant_dynamic-update-slice_fusion.3
  15.2 0.7 gather_fusion
  15.9 0.8 multiply_subtract_fusion.3
  16.7 2.5 collective-permute-done.1
  19.3 3.1 collective-permute-start.3
  22.5 1.3 collective-permute-start.2
  23.8 0.6 iota_compare_fusion.1
  24.4 0.2 collective-permute-done.3
  24.5 3.8 %collective-permute-done.2 = f32[12,18,1]{2,1,0:T(8,128)S(1)} collective-permute-done((f32[12,18,1]{2,1,0:T(8,128)S(1)}, f32[12,18,1]{2,1,0:T(8,128)S(1)}, u32[]{:S(2)}, u32[]{:S(2)}) %collective-permute-start.2) | collective-permute-done | bytes 896 | tf_op jit(solution)/shard_map/ppermute | solution.py:25
  28.4 4.2 %fusion.28 = (f32[1,12,16,2048]{3,2,1,0:T(8,128)}, f32[12,16,2048]{2,1,0:T(8,128)S(1)}) fusion(f32[12,16,2048]{2,1,0:T(8,128)S(1)} %copy-done.1, f32[16,2048]{1,0:T(8,128)S(1)} %get-tuple-element.28, f32[16,2048]{1,0:T(8,128)S(1)} %get-tuple-element.27, f32[12,1,2048]{2,1,0:T(1,128)} %copy-done.9, f32[12,1,2048]{2,1,0:T(1,128)} %copy-done.10, ...), kind=kLoop, calls=%fused_computation.115 | loop fusion | flops 9043968 | bytes 5310144 | tf_op jit(solution)/shard_map/stack | solution.py:107
  32.6 0.2 broadcast_multiply_fusion.2
  32.9 9.9 %collective-permute-start.4 = (f32[12,1,2048]{2,1,0:T(1,128)S(1)}, f32[12,1,2048]{2,1,0:T(1,128)S(1)}, u32[]{:S(2)}, u32[]{:S(2)}) collective-permute-start(f32[12,1,2048]{2,1,0:T(1,128)S(1)} %get-tuple-element.24), channel_id=1, source_target_pairs={{4,0},{8,4},{12,8},{16,12},{20,16},{24,20},{28,24},{32,28},{36,32}... | collective-permute-start | bytes 294920 | tf_op jit(solution)/shard_map/ppermute | solution.py:25
  42.8 1.9 collective-permute-start.5
  44.7 0.5 shift-left_bitcast_fusion
  45.2 1.1 collective-permute-done.5
  46.3 0.8 pad_maximum_fusion.41
  47.1 3.8 %collective-permute-start.7 = (f32[12,18,1]{2,1,0:T(8,128)}, f32[12,18,1]{2,1,0:T(8,128)}, u32[]{:S(2)}, u32[]{:S(2)}) collective-permute-start(f32[12,18,1]{2,1,0:T(8,128)} %get-tuple-element.16), channel_id=1, source_target_pairs={{0,1},{1,2},{2,3},{4,5},{5,6},{6,7},{8,9},{9,10},{10,11},{12,13},{... | collective-permute-start | bytes 2600 | tf_op jit(solution)/shard_map/ppermute | solution.py:22
  50.9 1.3 collective-permute-start.6
  52.2 0.5 fusion.22
  52.7 1.3 gather_fusion.1
  54.0 1.2 neg.16
  55.2 1.9 collective-permute-done.6
  57.1 5.9 %fusion.29 = (f32[1,12,16,2048]{3,2,1,0:T(8,128)S(1)}, f32[12,16,2048]{2,1,0:T(8,128)S(1)}) fusion(f32[12,16,2048]{2,1,0:T(8,128)S(1)} %get-tuple-element.6, f32[16,2048]{1,0:T(8,128)S(1)} %get-tuple-element.28, f32[16,2048]{1,0:T(8,128)S(1)} %get-tuple-element.27, f32[12,1,2048]{2,1,0:T(1,128)} %copy-done.7, f32[12,16,2048]{2,1,0:T(8,128)} %copy-done.2, ...), kind=kLoop, calls=%fused_computation.116 | loop fusion | flops 9043968 | bytes 6883008 | tf_op jit(solution)/shard_map/stack | solution.py:107
  63.0 0.2 broadcast_multiply_fusion.1
  63.2 0.1 fusion.32
  63.3 9.6 %collective-permute-start.8 = (f32[12,1,2048]{2,1,0:T(1,128)S(1)}, f32[12,1,2048]{2,1,0:T(1,128)S(1)}, u32[]{:S(2)}, u32[]{:S(2)}) collective-permute-start(f32[12,1,2048]{2,1,0:T(1,128)S(1)} %get-tuple-element.22), channel_id=1, source_target_pairs={{4,0},{8,4},{12,8},{16,12},{20,16},{24,20},{28,24},{32,28},{36,32}... | collective-permute-start | bytes 294920 | tf_op jit(solution)/shard_map/ppermute | solution.py:25
  73.0 1.9 collective-permute-start.9
  74.9 1.3 constant_dynamic-update-slice_fusion.2
  76.2 0.4 collective-permute-done.9
  76.7 2.2 collective-permute-start.11
  78.9 1.3 collective-permute-start.10
  80.2 1.3 constant_dynamic-update-slice_fusion.1
  81.5 3.3 collective-permute-done.10
  84.8 2.4 fusion.30
  87.4 9.1 %collective-permute-start.12 = (f32[12,1,2048]{2,1,0:T(1,128)S(1)}, f32[12,1,2048]{2,1,0:T(1,128)S(1)}, u32[]{:S(2)}, u32[]{:S(2)}) collective-permute-start(f32[12,1,2048]{2,1,0:T(1,128)S(1)} %get-tuple-element.20), channel_id=1, source_target_pairs={{4,0},{8,4},{12,8},{16,12},{20,16},{24,20},{28,24},{32,28},{36,32}... | collective-permute-start | bytes 294920 | tf_op jit(solution)/shard_map/ppermute | solution.py:25
  96.5 1.9 collective-permute-start.13
  98.4 0.2 constant_dynamic-update-slice_fusion
  98.6 1.4 collective-permute-done.13
  100.2 1.6 collective-permute-start.15
  101.8 1.3 collective-permute-start.14
  103.1 2.9 pad_maximum_fusion
  106.0 1.7 collective-permute-done.14
  107.7 2.6 bitcast_dynamic-update-slice_fusion
  110.3 0.6 pad.148
  110.9 5.0 %copy.32 = f32[8,8,16,2048]{3,1,2,0:T(8,128)S(1)} copy(f32[8,8,16,2048]{3,2,1,0:T(8,128)S(1)} %bitcast.80) | data formatting | bytes 16777216
  116.0 6.9 %fusion.35 = f32[60,60]{0,1:T(8,128)S(1)} fusion(f32[60,32768]{1,0:T(8,128)S(1)} %bitcast.79), kind=kOutput, calls=%fused_computation.123 | convolution fusion | flops 1415577600 | bytes 7878720 | tf_op jit(solution)/shard_map/dot_general | solution.py:108
  122.9 103.8 %psum.7 = f32[60,60]{0,1:T(8,128)S(1)} all-reduce(f32[60,60]{0,1:T(8,128)S(1)} %fusion.35), channel_id=1, replica_groups=mesh['gx'=128,'gy'=4] {'gx','gy'}, use_global_device_ids=true, to_apply=%region_0.0 | all-reduce | flops 3600 | bytes 28800 | tf_op jit(solution)/shard_map/psum | solution.py:109
  226.7 5.5 %cholesky.35 = f32[60,60]{1,0:T(8,128)S(1)} custom-call(f32[60,60]{1,0:T(8,128)S(1)} %fusion.11), custom_call_target="Cholesky" | custom-call | tf_op jit(solution)/shard_map/jit(cholesky)/cholesky | solution.py:110
  232.3 0.6 compare_reduce_fusion.1
  232.9 0.7 fusion.12
  233.6 0.9 fusion.13
  234.7 0.8 fusion.9
  235.7 52.8 %custom-call.12 = f32[6,96,96]{2,1,0:T(8,128)S(1)} custom-call(f32[6,96,96]{2,1,0:T(8,128)S(1)} %fusion.7), custom_call_target="Cholesky" | custom-call | tf_op jit(solution)/shard_map/vmap(jit(cholesky))/cholesky | solution.py:84
  288.7 44.2 %custom-call.13 = f32[6,1,96,96]{2,3,1,0:T(8,128)S(1)} custom-call(f32[6,1,96,96]{3,2,1,0:T(8,128)S(1)} %select_bitcast_fusion), custom_call_target="InvertDiagBlocksLowerTriangular" | custom-call | tf_op jit(solution)/shard_map/vmap()/triangular_solve | solution.py:86
  333.0 0.6 gather_fusion.3
  333.6 0.6 gather_fusion.2
  334.2 0.6 fusion.8
  334.9 0.4 fusion.5
  335.2 0.6 fusion.3
  336.0 9.6 %fusion = f32[12,16,2048]{2,0,1:T(8,128)S(1)} fusion(f32[12,48,1]{1,0,2:T(8,128)S(1)} %reshape.114, f32[6,8,16,2048]{3,2,1,0:T(8,128)} %bitcast.82), kind=kOutput, calls=%fused_computation.4 | convolution fusion | flops 226492416 | bytes 7866624 | tf_op jit(solution)/shard_map/dot_general | solution.py:113
  345.6 2.1 copy.23
  (71 shorter events, 1.8 us)
Async XLA Ops:
  0.0 15.2 %copy-start = (f32[6,2]{0,1:T(2,128)S(1)}, f32[6,2]{0,1:T(2,128)}, u32[]{:S(2)}) copy-start(f32[6,2]{0,1:T(2,128)} %param.9) | copy-start | bytes 148
  1.5 15.1 %collective-permute-start = (f32[12,1,2048]{2,1,0:T(1,128)S(1)}, f32[12,1,2048]{2,1,0:T(1,128)S(1)}, u32[]{:S(2)}, u32[]{:S(2)}) collective-permute-start(f32[12,1,2048]{2,1,0:T(1,128)S(1)} %get-tuple-element.26), channel_id=1, source_target_pairs={{4,0},{8,4},{12,8},{16,12},{20,16},{24,20},{28,24},{32,28},{36,32}... | collective-permute-start | bytes 294920 | tf_op jit(solution)/shard_map/ppermute | solution.py:25
  10.3 4.9 %copy-start.11 = (f32[2,16,2048]{2,1,0:T(8,128)S(1)}, f32[2,16,2048]{2,1,0:T(8,128)}, u32[]{:S(2)}) copy-start(f32[2,16,2048]{2,1,0:T(8,128)} %param.8) | copy-start | bytes 786436
  10.3 5.6 %copy-start.15 = (f32[60,48]{0,1:T(8,128)S(1)}, f32[60,48]{0,1:T(8,128)}, u32[]{:S(2)}) copy-start(f32[60,48]{0,1:T(8,128)} %constant.126.clone) | copy-start | bytes 34564
  10.3 5.6 %copy-start.16 = (f32[60,48]{0,1:T(8,128)S(1)}, f32[60,48]{0,1:T(8,128)}, u32[]{:S(2)}) copy-start(f32[60,48]{0,1:T(8,128)} %constant.125.clone) | copy-start | bytes 34564
  10.3 8.9 %copy-start.1 = (f32[12,16,2048]{2,1,0:T(8,128)S(1)}, f32[12,16,2048]{2,1,0:T(8,128)}, u32[]{:S(2)}) copy-start(f32[12,16,2048]{2,1,0:T(8,128)} %param.6) | copy-start | bytes 4718596
  10.3 8.9 %collective-permute-start.1 = (f32[12,1,2048]{2,1,0:T(1,128)S(1)}, f32[12,1,2048]{2,1,0:T(1,128)S(1)}, u32[]{:S(2)}, u32[]{:S(2)}) collective-permute-start(f32[12,1,2048]{2,1,0:T(1,128)S(1)} %get-tuple-element.25), channel_id=1, source_target_pairs={{0,4},{4,8},{8,12},{12,16},{16,20},{20,24},{24,28},{28,32},{32,36}... | collective-permute-start | bytes 294920 | tf_op jit(solution)/shard_map/ppermute | solution.py:22
  15.1 13.2 %copy-start.5 = (f32[16,2048]{1,0:T(8,128)S(1)}, f32[16,2048]{1,0:T(8,128)}, u32[]{:S(2)}) copy-start(f32[16,2048]{1,0:T(8,128)} %param.7) | copy-start | bytes 393220
  16.7 11.7 %copy-start.9 = (f32[12,1,2048]{2,1,0:T(1,128)}, f32[12,1,2048]{2,1,0:T(1,128)S(1)}, u32[]{:S(2)}) copy-start(f32[12,1,2048]{2,1,0:T(1,128)S(1)} %collective-permute-done) | copy-start | bytes 294916
  19.2 9.2 %copy-start.10 = (f32[12,1,2048]{2,1,0:T(1,128)}, f32[12,1,2048]{2,1,0:T(1,128)S(1)}, u32[]{:S(2)}) copy-start(f32[12,1,2048]{2,1,0:T(1,128)S(1)} %collective-permute-done.1) | copy-start | bytes 294916
  19.3 5.2 %collective-permute-start.3 = (f32[12,18,1]{2,1,0:T(8,128)S(1)}, f32[12,18,1]{2,1,0:T(8,128)S(1)}, u32[]{:S(2)}, u32[]{:S(2)}) collective-permute-start(f32[12,18,1]{2,1,0:T(8,128)S(1)} %get-tuple-element.18), channel_id=1, source_target_pairs={{0,1},{1,2},{2,3},{4,5},{5,6},{6,7},{8,9},{9,10},{10,11},{12,13},{... | collective-permute-start | bytes 2600 | tf_op jit(solution)/shard_map/ppermute | solution.py:22
  22.5 5.9 %collective-permute-start.2 = (f32[12,18,1]{2,1,0:T(8,128)S(1)}, f32[12,18,1]{2,1,0:T(8,128)S(1)}, u32[]{:S(2)}, u32[]{:S(2)}) collective-permute-start(f32[12,18,1]{2,1,0:T(8,128)S(1)} %get-tuple-element.17), channel_id=1, source_target_pairs={{1,0},{2,1},{3,2},{5,4},{6,5},{7,6},{9,8},{10,9},{11,10},{13,12},{... | collective-permute-start | bytes 2600 | tf_op jit(solution)/shard_map/ppermute | solution.py:25
  32.7 13.6 %copy-start.2 = (f32[12,16,2048]{2,1,0:T(8,128)}, f32[12,16,2048]{2,1,0:T(8,128)S(1)}, u32[]{:S(2)}) copy-start(f32[12,16,2048]{2,1,0:T(8,128)S(1)} %broadcast_multiply_fusion.2) | copy-start | bytes 4718596
  32.9 12.4 %collective-permute-start.4 = (f32[12,1,2048]{2,1,0:T(1,128)S(1)}, f32[12,1,2048]{2,1,0:T(1,128)S(1)}, u32[]{:S(2)}, u32[]{:S(2)}) collective-permute-start(f32[12,1,2048]{2,1,0:T(1,128)S(1)} %get-tuple-element.24), channel_id=1, source_target_pairs={{4,0},{8,4},{12,8},{16,12},{20,16},{24,20},{28,24},{32,28},{36,32}... | collective-permute-start | bytes 294920 | tf_op jit(solution)/shard_map/ppermute | solution.py:25
  42.8 3.5 %collective-permute-start.5 = (f32[12,1,2048]{2,1,0:T(1,128)S(1)}, f32[12,1,2048]{2,1,0:T(1,128)S(1)}, u32[]{:S(2)}, u32[]{:S(2)}) collective-permute-start(f32[12,1,2048]{2,1,0:T(1,128)S(1)} %get-tuple-element.23), channel_id=1, source_target_pairs={{0,4},{4,8},{8,12},{12,16},{16,20},{20,24},{24,28},{28,32},{32,36}... | collective-permute-start | bytes 294920 | tf_op jit(solution)/shard_map/ppermute | solution.py:22
  45.2 1.9 copy-start.7
  46.3 0.8 copy-start.8
  47.1 8.0 %collective-permute-start.7 = (f32[12,18,1]{2,1,0:T(8,128)}, f32[12,18,1]{2,1,0:T(8,128)}, u32[]{:S(2)}, u32[]{:S(2)}) collective-permute-start(f32[12,18,1]{2,1,0:T(8,128)} %get-tuple-element.16), channel_id=1, source_target_pairs={{0,1},{1,2},{2,3},{4,5},{5,6},{6,7},{8,9},{9,10},{10,11},{12,13},{... | collective-permute-start | bytes 2600 | tf_op jit(solution)/shard_map/ppermute | solution.py:22
  50.9 6.2 %collective-permute-start.6 = (f32[12,18,1]{2,1,0:T(8,128)}, f32[12,18,1]{2,1,0:T(8,128)}, u32[]{:S(2)}, u32[]{:S(2)}) collective-permute-start(f32[12,18,1]{2,1,0:T(8,128)} %get-tuple-element.15), channel_id=1, source_target_pairs={{1,0},{2,1},{3,2},{5,4},{6,5},{7,6},{9,8},{10,9},{11,10},{13,12},{... | collective-permute-start | bytes 2600 | tf_op jit(solution)/shard_map/ppermute | solution.py:25
  63.3 12.8 %collective-permute-start.8 = (f32[12,1,2048]{2,1,0:T(1,128)S(1)}, f32[12,1,2048]{2,1,0:T(1,128)S(1)}, u32[]{:S(2)}, u32[]{:S(2)}) collective-permute-start(f32[12,1,2048]{2,1,0:T(1,128)S(1)} %get-tuple-element.22), channel_id=1, source_target_pairs={{4,0},{8,4},{12,8},{16,12},{20,16},{24,20},{28,24},{32,28},{36,32}... | collective-permute-start | bytes 294920 | tf_op jit(solution)/shard_map/ppermute | solution.py:25
  73.0 3.5 %collective-permute-start.9 = (f32[12,1,2048]{2,1,0:T(1,128)S(1)}, f32[12,1,2048]{2,1,0:T(1,128)S(1)}, u32[]{:S(2)}, u32[]{:S(2)}) collective-permute-start(f32[12,1,2048]{2,1,0:T(1,128)S(1)} %get-tuple-element.21), channel_id=1, source_target_pairs={{0,4},{4,8},{8,12},{12,16},{16,20},{20,24},{24,28},{28,32},{32,36}... | collective-permute-start | bytes 294920 | tf_op jit(solution)/shard_map/ppermute | solution.py:22
  76.7 4.8 %collective-permute-start.11 = (f32[12,18,1]{2,1,0:T(8,128)S(1)}, f32[12,18,1]{2,1,0:T(8,128)S(1)}, u32[]{:S(2)}, u32[]{:S(2)}) collective-permute-start(f32[12,18,1]{2,1,0:T(8,128)S(1)} %get-tuple-element.14), channel_id=1, source_target_pairs={{0,1},{1,2},{2,3},{4,5},{5,6},{6,7},{8,9},{9,10},{10,11},{12,13},{... | collective-permute-start | bytes 2600 | tf_op jit(solution)/shard_map/ppermute | solution.py:22
  78.9 5.9 %collective-permute-start.10 = (f32[12,18,1]{2,1,0:T(8,128)S(1)}, f32[12,18,1]{2,1,0:T(8,128)S(1)}, u32[]{:S(2)}, u32[]{:S(2)}) collective-permute-start(f32[12,18,1]{2,1,0:T(8,128)S(1)} %get-tuple-element.13), channel_id=1, source_target_pairs={{1,0},{2,1},{3,2},{5,4},{6,5},{7,6},{9,8},{10,9},{11,10},{13,12},{... | collective-permute-start | bytes 2600 | tf_op jit(solution)/shard_map/ppermute | solution.py:25
  84.8 13.6 %copy-start.3 = (f32[5,12,16,2048]{3,2,1,0:T(8,128)S(1)}, f32[5,12,16,2048]{3,2,1,0:T(8,128)}, u32[]{:S(2)}) copy-start(f32[5,12,16,2048]{3,2,1,0:T(8,128)} %constant_dynamic-update-slice_fusion.1) | copy-start | bytes 23592964
  87.4 11.2 %collective-permute-start.12 = (f32[12,1,2048]{2,1,0:T(1,128)S(1)}, f32[12,1,2048]{2,1,0:T(1,128)S(1)}, u32[]{:S(2)}, u32[]{:S(2)}) collective-permute-start(f32[12,1,2048]{2,1,0:T(1,128)S(1)} %get-tuple-element.20), channel_id=1, source_target_pairs={{4,0},{8,4},{12,8},{16,12},{20,16},{24,20},{28,24},{32,28},{36,32}... | collective-permute-start | bytes 294920 | tf_op jit(solution)/shard_map/ppermute | solution.py:25
  96.5 3.5 %collective-permute-start.13 = (f32[12,1,2048]{2,1,0:T(1,128)S(1)}, f32[12,1,2048]{2,1,0:T(1,128)S(1)}, u32[]{:S(2)}, u32[]{:S(2)}) collective-permute-start(f32[12,1,2048]{2,1,0:T(1,128)S(1)} %get-tuple-element.19), channel_id=1, source_target_pairs={{0,4},{4,8},{8,12},{12,16},{16,20},{20,24},{24,28},{28,32},{32,36}... | collective-permute-start | bytes 294920 | tf_op jit(solution)/shard_map/ppermute | solution.py:22
  98.6 4.5 %copy-start.4 = (f32[1,12,16,2048]{3,2,1,0:T(8,128)S(1)}, f32[1,12,16,2048]{3,2,1,0:T(8,128)}, u32[]{:S(2)}) copy-start(f32[1,12,16,2048]{3,2,1,0:T(8,128)} %get-tuple-element.5) | copy-start | bytes 4718596
  100.2 5.9 %collective-permute-start.15 = (f32[12,18,1]{2,1,0:T(8,128)S(1)}, f32[12,18,1]{2,1,0:T(8,128)S(1)}, u32[]{:S(2)}, u32[]{:S(2)}) collective-permute-start(f32[12,18,1]{2,1,0:T(8,128)S(1)} %get-tuple-element.12), channel_id=1, source_target_pairs={{0,1},{1,2},{2,3},{4,5},{5,6},{6,7},{8,9},{9,10},{10,11},{12,13},{... | collective-permute-start | bytes 2600 | tf_op jit(solution)/shard_map/ppermute | solution.py:22
  101.8 5.9 %collective-permute-start.14 = (f32[12,18,1]{2,1,0:T(8,128)S(1)}, f32[12,18,1]{2,1,0:T(8,128)S(1)}, u32[]{:S(2)}, u32[]{:S(2)}) collective-permute-start(f32[12,18,1]{2,1,0:T(8,128)S(1)} %get-tuple-element.11), channel_id=1, source_target_pairs={{1,0},{2,1},{3,2},{5,4},{6,5},{7,6},{9,8},{10,9},{11,10},{13,12},{... | collective-permute-start | bytes 2600 | tf_op jit(solution)/shard_map/ppermute | solution.py:25
  116.0 117.6 %copy-start.6 = (f32[6,60,48]{1,2,0:T(8,128)S(1)}, f32[6,60,48]{1,2,0:T(8,128)}, u32[]{:S(2)}) copy-start(f32[6,60,48]{1,2,0:T(8,128)} %multiply_subtract_fusion.3) | copy-start | bytes 207364
  116.0 118.5 %copy-start.17 = (f32[6]{0:T(128)S(1)}, f32[6]{0:T(128)}, u32[]{:S(2)}) copy-start(f32[6]{0:T(128)} %neg.16) | copy-start | bytes 76
  233.6 55.0 %copy-start.12 = (pred[96,96]{1,0:T(8,128)(4,1)S(1)}, pred[96,96]{1,0:T(8,128)(4,1)}, u32[]{:S(2)}) copy-start(pred[96,96]{1,0:T(8,128)(4,1)} %iota_compare_fusion.1) | copy-start | bytes 27652
  234.6 98.3 %copy-start.13 = (s32[6]{0:T(128)S(1)}, s32[6]{0:T(128)}, u32[]{:S(2)}) copy-start(s32[6]{0:T(128)} %shift-left_bitcast_fusion) | copy-start | bytes 76
  234.6 98.9 %copy-start.14 = (s32[6]{0:T(128)S(1)}, s32[6]{0:T(128)}, u32[]{:S(2)}) copy-start(s32[6]{0:T(128)} %fusion.22) | copy-start | bytes 76
where the time goes:
time: 348 us
  other arithmetic  130 us (37%)
  blocking collectives  104 us (30%)
  starting transfers between devices  61 us (18%)
  matrix products  19.8 us (6%)
  waiting for transfers between devices  16.2 us (5%)
  local copies, waits for them, and re-layouts  16 us (5%)
    psum x1, blocking collectives, per_device(): global_gram = lax.psum(local_gram, ('gx', 'gy'))  104 us
    another operation x4, other arithmetic, single(): factor = jnp.linalg.cholesky(normal)  52.9 us
    another operation x3, other arithmetic, single(): lax.linalg.triangular_solve(factor, middle, left_side=True, lower=True, t...  45 us
    ppermute x8, starting transfers between devices, padded_2(): lax.ppermute(lax.slice_in_dim(block, 0, width, axis=dim), axis, backward)  42.5 us
    ppermute x8, starting transfers between devices, padded_2(): lax.ppermute(lax.slice_in_dim(block, block.shape[dim] - width, None, axis...  18.5 us
    another operation x5, other arithmetic, per_device(): jnp.stack(krylov).reshape(len(krylov) * channels, tile_rows * tile_cols)  18 us
    ppermute x8, waiting for transfers between devices, padded_2(): lax.ppermute(lax.slice_in_dim(block, 0, width, axis=dim), axis, backward)  10.7 us
    dot_general x1, matrix products, per_device(): solution = jnp.dot(mixing, basis_rows[:columns], precision=highest)  9.59 us
  transfers between devices with their start and end apart: 16, of which 9 were waited for; matrix products, arithmetic and copies ran while one was open for 4% of the time, Pallas kernels for 0%

commit v1 on v0

v1 whole, which is shorter than its diff:
```python
import functools

import jax
import jax.numpy as jnp
import numpy as np
from jax import lax
from jax.experimental import pallas as pl
from jax.experimental.pallas import tpu as pltpu
from jax.sharding import Mesh
from jax.sharding import PartitionSpec as P

S = 4
THETA = (-8.0, -2.0, -14.0, -5.0)
SCALE = 8.0
CH = 12
HALO = 4
LANE = 128
HIGH = lax.Precision.HIGHEST
F32 = jnp.float32
BF16 = jnp.bfloat16
HI_AT = (0, 16, 32, 48, 128)
LO_AT = (64, 80, 96, 112, 144)
ROWS = 160


def selection():
    pick = np.zeros((64, ROWS), np.float32)
    for k in range(S + 1):
        for c in range(CH):
            i = k * CH + c
            at = i if i < 30 else i + 2
            pick[at, HI_AT[k] + c] = 1.0
            pick[at, LO_AT[k] + c] = 1.0
    return pick


def expansion():
    spread = np.zeros((64, 48), np.float32)
    for k in range(S):
        for c in range(CH):
            spread[k * 16 + c, k * CH + c] = 1.0
    return spread


def split(value):
    high = value.astype(BF16)
    return high, (value - high.astype(F32)).astype(BF16)


def krylov_kernel(own, low, high, side, pick, basis, gram, va, vb, coef, acc, *, tile_rows, tile_cols):
    wide = tile_cols + LANE
    depth = tile_rows + 2 * HALO

    def load(r, src, at):
        va[r, :, :, :tile_cols] = src[at]
        va[r, :, :, tile_cols:] = side[r]

    def fill_low(i, _):
        load(i, low, i)
        return 0

    def fill_high(i, _):
        load(i + HALO + tile_rows, high, i)
        return 0

    def keep(k, r, value):
        hi, lo = split(value[:, :, :tile_cols].reshape(16, tile_cols))
        basis[r, HI_AT[k] : HI_AT[k] + 16, :] = hi
        basis[r, LO_AT[k] : LO_AT[k] + 16, :] = lo

    def fill_own(i, _):
        load(i + HALO, own, i)
        keep(0, i, own[i])
        return 0

    lax.fori_loop(0, HALO, fill_low, 0)
    lax.fori_loop(0, HALO, fill_high, 0)
    lax.fori_loop(0, tile_rows, fill_own, 0)

    def coefficients(r, _):
        spread = jnp.broadcast_to(va[r, 1, 4:5, :], (8, wide)) * (1.0 / SCALE)
        drift_x = jnp.broadcast_to(va[r, 1, 5:6, :], (8, wide)) * (0.5 / SCALE)
        drift_y = jnp.broadcast_to(va[r, 1, 6:7, :], (8, wide)) * (0.5 / SCALE)
        coef[r, 0] = spread + drift_x
        coef[r, 1] = spread - drift_x
        coef[r, 2] = spread + drift_y
        coef[r, 3] = spread - drift_y
        coef[r, 4] = -4.0 * spread
        return 0

    lax.fori_loop(1, depth - 1, coefficients, 0)

    bufs = (va, vb)
    for k in range(S):
        src, dst = bufs[k % 2], bufs[(k + 1) % 2]

        def advance(r, k=k, src=src, dst=dst):
            center = src[r]
            value = (
                coef[r, 0][None] * src[r + 1]
                + coef[r, 1][None] * src[r - 1]
                + coef[r, 2][None] * pltpu.roll(center, wide - 1, 2)
                + coef[r, 3][None] * pltpu.roll(center, 1, 2)
                + (coef[r, 4] - THETA[k] / SCALE)[None] * center
            )
            if k < S - 1:
                dst[r] = value
            return value

        def outer(r, _, advance=advance):
            advance(r)
            return 0

        def inner(i, _, k=k, advance=advance):
            keep(k + 1, i, advance(i + HALO))
            return 0

        if k < S - 1:
            lax.fori_loop(k + 1, HALO, outer, 0)
            lax.fori_loop(HALO + tile_rows, depth - 1 - k, outer, 0)
        lax.fori_loop(0, tile_rows, inner, 0)

    acc[...] = jnp.zeros_like(acc)

    def accumulate(i, _):
        rows = basis[i]
        acc[...] += lax.dot_general(rows, rows, (((1,), (1,)), ((), ())), preferred_element_type=F32)
        return 0

    lax.fori_loop(0, tile_rows, accumulate, 0)
    half = jnp.dot(pick[...], acc[...], precision=HIGH, preferred_element_type=F32)
    gram[...] = lax.dot_general(half, pick[...], (((1,), (1,)), ((), ())), precision=HIGH, preferred_element_type=F32)


def lane(shape):
    return lax.broadcasted_iota(jnp.int32, shape, len(shape) - 1)


def solve_kernel(shifts, gram, spread, basis_hbm, out, basis, mixed, sem, *, tile_rows, tile_cols):
    copy = pltpu.make_async_copy(basis_hbm.at[:, 0:128, :], basis, sem)
    copy.start()

    g = gram[...]
    lanes = lane((48, 2 * 64))
    theta_col = jnp.zeros((48, 128), F32)
    theta_row = jnp.zeros((48, 128), F32)
    rows_id = lax.broadcasted_iota(jnp.int32, (48, 128), 0)
    for k in range(S):
        theta_row = jnp.where((rows_id >= 12 * k) & (rows_id < 12 * k + 12), THETA[k], theta_row)
        theta_col = jnp.where((lanes >= 12 * k) & (lanes < 12 * k + 12), THETA[k], theta_col)
    g0 = g[0:48]
    gd = pltpu.roll(g, 64 - 12, 0)[0:48]
    gr = pltpu.roll(g0, 128 - 12, 1)
    grd = pltpu.roll(gd, 128 - 12, 1)
    inside = lanes < 48
    at_rhs = lanes == 48
    systems = []
    for j in range(CH // 2):
        a = shifts[j, 0]
        b = shifts[j, 1]
        alpha_i = theta_row - a
        alpha_l = theta_col - a
        real = (alpha_i * alpha_l + b * b) * g0 + SCALE * (alpha_i * gr + alpha_l * gd) + SCALE * SCALE * grd
        imag = b * ((alpha_l - alpha_i) * g0 + SCALE * (gr - gd))
        g1 = pltpu.roll(g0, 48 - 2 * j, 1)
        g2 = pltpu.roll(g0, 47 - 2 * j, 1)
        gd1 = pltpu.roll(gd, 48 - 2 * j, 1)
        gd2 = pltpu.roll(gd, 47 - 2 * j, 1)
        rhs_real = alpha_i * g1 - b * g2 + SCALE * gd1
        rhs_imag = alpha_i * g2 + b * g1 + SCALE * gd2
        real = jnp.where(inside, real, jnp.where(at_rhs, rhs_real, 0.0))
        imag = jnp.where(inside, imag, jnp.where(at_rhs, rhs_imag, 0.0))
        systems.append(real + pltpu.roll(imag, 64, 1))

    flip = jnp.where(lane((1, 128)) < 64, -1.0, 1.0)
    for k in range(48):
        for j in range(CH // 2):
            m = systems[j]
            col_real = jnp.broadcast_to(m[:, k : k + 1], (48, 128))
            col_imag = jnp.broadcast_to(m[:, 64 + k : 65 + k], (48, 128))
            inverse = 1.0 / col_real[k : k + 1, :]
            row = m[k : k + 1, :] * inverse
            turned = pltpu.roll(row, 64, 1) * flip
            pivot = rows_id == k
            update = m - col_real * row - col_imag * turned
            systems[j] = jnp.where(pivot, jnp.broadcast_to(row, (48, 128)), update)

    mix = jnp.zeros((48, 128), F32)
    for j in range(CH // 2):
        m = systems[j]
        mix = jnp.where(lanes == 2 * j, jnp.broadcast_to(m[:, 48:49], (48, 128)), mix)
        mix = jnp.where(lanes == 2 * j + 1, jnp.broadcast_to(m[:, 112:113], (48, 128)), mix)
    mix = jnp.dot(spread[...], mix, precision=HIGH, preferred_element_type=F32)
    mix_hi, mix_lo = split(mix)
    weights = mix_hi.astype(F32) + pltpu.roll(mix_lo.astype(F32), 16, 1)
    weights = jnp.concatenate([weights, weights], axis=0).T[0:32].astype(BF16)

    copy.wait()

    def combine(i, _):
        both = jnp.dot(weights, basis[i], preferred_element_type=F32)
        mixed[i] = both[0:16] + both[16:32]
        return 0

    lax.fori_loop(0, tile_rows, combine, 0)
    out[...] = mixed[:, 0:CH, :]


def per_device(right_side, diffusion, drift_field, shifts):
    tile_rows, tile_cols = right_side.shape[1:]
    fields = jnp.concatenate(
        [right_side, diffusion[None], drift_field, jnp.zeros((1, tile_rows, tile_cols), F32)], axis=0
    )
    fields = fields.transpose(1, 0, 2)
    gx = ("z", "y", "core")
    count = lax.axis_size(gx)
    ring_up = [(i, (i + 1) % count) for i in range(count)]
    ring_down = [(i, (i - 1) % count) for i in range(count)]
    low = lax.ppermute(fields[-HALO:], gx, ring_up)
    high = lax.ppermute(fields[:HALO], gx, ring_down)
    gy = lax.axis_size("x")
    edge_right = jnp.concatenate([p[:, :, -LANE:] for p in (low, fields, high)], axis=0)
    edge_left = jnp.concatenate([p[:, :, :LANE] for p in (low, fields, high)], axis=0)
    from_left = lax.ppermute(edge_right, "x", [(i, i + 1) for i in range(gy - 1)])
    from_right = lax.ppermute(edge_left, "x", [(i + 1, i) for i in range(gy - 1)])
    side = jnp.where(lax.broadcasted_iota(jnp.int32, from_left.shape, 2) < LANE // 2, from_right, from_left)

    def halves(x):
        return x.reshape(x.shape[0], 2, 8, x.shape[2])

    wide, depth = tile_cols + LANE, tile_rows + 2 * HALO
    basis, gram = pl.pallas_call(
        functools.partial(krylov_kernel, tile_rows=tile_rows, tile_cols=tile_cols),
        out_shape=(
            jax.ShapeDtypeStruct((tile_rows, ROWS, tile_cols), BF16),
            jax.ShapeDtypeStruct((64, 64), F32),
        ),
        scratch_shapes=[
            pltpu.VMEM((depth, 2, 8, wide), F32),
            pltpu.VMEM((depth, 2, 8, wide), F32),
            pltpu.VMEM((depth, 5, 8, wide), F32),
            pltpu.VMEM((ROWS, ROWS), F32),
        ],
        compiler_params=pltpu.CompilerParams(vmem_limit_bytes=60 * 2**20),
        name="krylov",
    )(halves(fields), halves(low), halves(high), halves(side), jnp.asarray(selection()))

    first, cross, second = gram[:32, :32], gram[:32, 32:], gram[32:, 32:]
    row = lax.broadcasted_iota(jnp.int32, (32, 32), 0)
    column = lax.broadcasted_iota(jnp.int32, (32, 32), 1)
    packed = jnp.where(row >= column, first, second)
    diagonal = jnp.sum(jnp.where(row == column, second, 0.0), axis=1, keepdims=True)
    packed = jnp.where(column == 31, diagonal, packed)
    payload = jnp.concatenate([cross, packed], axis=1)
    payload = jnp.concatenate([payload[:16], payload[16:]], axis=1)
    for axes in (("y", "core", "x"), ("z",)):
        members = lax.axis_size(axes)
        parts = lax.all_to_all(jnp.broadcast_to(payload[None], (members, 16, LANE)), axes, 0, 0, tiled=True)
        payload = jnp.sum(parts, axis=0)
    payload = jnp.concatenate([payload[:, :64], payload[:, 64:]], axis=0)
    cross, packed = payload[:30, :30], payload[:30, 32:62]
    diagonal = payload[:30, 63]
    row, column = row[:30, :30], column[:30, :30]
    first = jnp.where(row >= column, packed, packed.T)
    second = jnp.where(row < column, packed, packed.T)
    second = jnp.where(row == column, diagonal[None], second)
    gram = jnp.concatenate(
        [jnp.concatenate([first, cross], axis=1), jnp.concatenate([cross.T, second], axis=1)], axis=0
    )
    gram = jnp.pad(gram, ((0, 4), (0, 68)))

    out = pl.pallas_call(
        functools.partial(solve_kernel, tile_rows=tile_rows, tile_cols=tile_cols),
        out_shape=jax.ShapeDtypeStruct((tile_rows, CH, tile_cols), F32),
        in_specs=[
            pl.BlockSpec(memory_space=pltpu.SMEM),
            pl.BlockSpec(memory_space=pltpu.VMEM),
            pl.BlockSpec(memory_space=pltpu.VMEM),
            pl.BlockSpec(memory_space=pl.ANY),
        ],
        scratch_shapes=[
            pltpu.VMEM((tile_rows, 128, tile_cols), BF16),
            pltpu.VMEM((tile_rows, 16, tile_cols), F32),
            pltpu.SemaphoreType.DMA,
        ],
        compiler_params=pltpu.CompilerParams(vmem_limit_bytes=60 * 2**20),
        name="solve",
    )(shifts, gram, jnp.asarray(expansion()), basis)
    return out.transpose(1, 0, 2)


def solution(mesh):
    fine = Mesh(mesh.devices.reshape(16, 4, 2, 4), ("z", "y", "core", "x"))
    gx = ("z", "y", "core")
    in_specs = (P(None, gx, "x"), P(gx, "x"), P(None, gx, "x"), P())
    return jax.shard_map(
        per_device, mesh=fine, in_specs=in_specs, out_specs=P(None, gx, "x"), check_vma=False
    )
```

time: 348 us -> 125 us (0.36)
  other arithmetic: 130 us -> 4.94 us
  blocking collectives: 104 us -> 22.6 us
  Pallas kernels: 0 us -> 44 us
  starting transfers between devices: 61 us -> 24.8 us
  matrix products: 19.8 us -> 0 us
  local copies, waits for them, and re-layouts: 16 us -> 11.1 us
    another operation x16 -> x0, other arithmetic: 122 us -> none  [the longest x4 52.9 us: single(): factor = jnp.linalg.cholesky(normal)]
    psum x1 -> x0, blocking collectives: 104 us -> none  [per_device(): global_gram = lax.psum(local_gram, ('gx', 'gy'))]
    ppermute x16 -> x4, starting transfers between devices: 61 us -> 15.1 us  [the longest x1 6.08 us: per_device(): high = lax.ppermute(fields[:HALO], gx, ring_down)]
    pallas_call x0 -> x2, Pallas kernels: none -> 44 us  [the longest x1 24.2 us: per_device(): pl.pallas_call(functools.partial(krylov_kernel, tile_rows=tile_rows, tile...]
    all_to_all x0 -> x1, blocking collectives: none -> 22.6 us  [per_device(): lax.all_to_all(jnp.broadcast_to(payload[None], (members, 16, LANE)), axes...]
    dot_general x4 -> x0, matrix products: 17.9 us -> none  [the longest x1 9.59 us: per_device(): solution = jnp.dot(mixing, basis_rows[:columns], precision=highest)]
    ppermute x16 -> x4, waiting for transfers between devices: 16.2 us -> 4.7 us  [the longest x1 2.87 us: per_device(): lax.ppermute(edge_left, 'x', [(i + 1, i) for i in range(gy - 1)])]
    all_to_all x0 -> x1, waiting for transfers between devices: none -> 11.4 us  [per_device(): lax.all_to_all(jnp.broadcast_to(payload[None], (members, 16, LANE)), axes...]
  transfers between devices with their start and end apart: 16 -> 5, of which waited for: 9 -> 3; matrix products, arithmetic and copies ran while one was open for 4% -> 4% of each run, Pallas kernels for 0% -> 0%
where the time goes in v1:
time: 125 us; the launch traced here: 124 us
  Pallas kernels  44 us (35%)
  starting transfers between devices  24.8 us (20%)
  blocking collectives  22.6 us (18%)
  waiting for transfers between devices  16.1 us (13%)
  local copies, waits for them, and re-layouts  11.1 us (9%)
  other arithmetic  4.94 us (4%)
    pallas_call x1, Pallas kernels, per_device(): pl.pallas_call(functools.partial(krylov_kernel, tile_rows=tile_rows, tile...  24.2 us
    all_to_all x1, blocking collectives, per_device(): lax.all_to_all(jnp.broadcast_to(payload[None], (members, 16, LANE)), axes...  22.6 us
    pallas_call x1, Pallas kernels, per_device(): pl.pallas_call(functools.partial(solve_kernel, tile_rows=tile_rows, tile_...  19.8 us
    all_to_all x1, waiting for transfers between devices, per_device(): lax.all_to_all(jnp.broadcast_to(payload[None], (members, 16, LANE)), axes...  11.4 us
    all_to_all x1, starting transfers between devices, per_device(): lax.all_to_all(jnp.broadcast_to(payload[None], (members, 16, LANE)), axes...  9.72 us
    ppermute x1, starting transfers between devices, per_device(): high = lax.ppermute(fields[:HALO], gx, ring_down)  6.08 us
    ppermute x1, starting transfers between devices, per_device(): low = lax.ppermute(fields[-HALO:], gx, ring_up)  4.58 us
    transpose x1, local copies, waits for them, and re-layouts, per_device(): return out.transpose(1, 0, 2)  3.65 us
  transfers between devices with their start and end apart: 5, of which 3 were waited for; matrix products, arithmetic and copies ran while one was open for 4% of the time, Pallas kernels for 0%

profile of v1, /device:TPU:1, one launch (start us, length us, event | category | flops | bytes accessed | tf_op | source)
XLA Modules:
  0.0 123.7 jit_solution(8701617898675654072)
XLA Ops:
  0.0 0.1 pad.24.clone
  0.1 1.9 %maximum_bitcast_fusion = f32[16,16,2048]{2,0,1:T(8,128)S(1)} fusion(f32[2,16,2048]{2,1,0:T(8,128)} %param.8, f32[1,16,2048]{2,1,0:T(8,128)} %bitcast.30, f32[12,16,2048]{2,1,0:T(8,128)} %param.6, f32[16]{0:T(128)S(1)} %pad.24.clone), kind=kLoop, calls=%fused_computation | loop fusion | flops 1572864 | bytes 4063296 | tf_op jit(solution)/shard_map/transpose | solution.py:214
  2.0 0.2 fusion.11
  2.2 4.6 %collective-permute-start = (f32[4,16,2048]{2,0,1:T(4,128)S(1)}, f32[4,16,2048]{2,0,1:T(4,128)S(1)}, u32[]{:S(2)}, u32[]{:S(2)}) collective-permute-start(f32[4,16,2048]{2,0,1:T(4,128)S(1)} %get-tuple-element.12), channel_id=1, source_target_pairs={{0,4},{4,8},{8,12},{12,16},{16,20},{20,24},{24,28},{28,32},{32,36}... | collective-permute-start | bytes 1572872 | tf_op jit(solution)/shard_map/ppermute | solution.py:219
  6.8 6.1 %collective-permute-start.1 = (f32[4,16,2048]{2,0,1:T(4,128)S(1)}, f32[4,16,2048]{2,0,1:T(4,128)S(1)}, u32[]{:S(2)}, u32[]{:S(2)}) collective-permute-start(f32[4,16,2048]{2,0,1:T(4,128)S(1)} %get-tuple-element.11), channel_id=1, source_target_pairs={{0,508},{4,0},{8,4},{12,8},{16,12},{20,16},{24,20},{28,24},{32,28}... | collective-permute-start | bytes 1572872 | tf_op jit(solution)/shard_map/ppermute | solution.py:220
  12.9 2.5 %copy.35 = f32[16,16,2048]{2,1,0:T(8,128)} copy(f32[16,16,2048]{2,0,1:T(8,128)S(1)} %maximum_bitcast_fusion) | data formatting | bytes 4194304 | tf_op jit(solution)/shard_map/transpose | solution.py:214
  15.4 0.0 collective-permute-done
  15.5 1.8 %collective-permute-done.1 = f32[4,16,2048]{2,0,1:T(4,128)S(1)} collective-permute-done((f32[4,16,2048]{2,0,1:T(4,128)S(1)}, f32[4,16,2048]{2,0,1:T(4,128)S(1)}, u32[]{:S(2)}, u32[]{:S(2)}) %collective-permute-start.1) | collective-permute-done | bytes 524320 | tf_op jit(solution)/shard_map/ppermute | solution.py:220
  17.3 3.1 %collective-permute-start.3 = (f32[24,16,128]{2,0,1:T(8,128)S(1)}, f32[24,16,128]{2,0,1:T(8,128)S(1)}, u32[]{:S(2)}, u32[]{:S(2)}) collective-permute-start(f32[24,16,128]{2,0,1:T(8,128)S(1)} %pad_maximum_fusion.1), channel_id=1, source_target_pairs={{0,1},{1,2},{2,3},{4,5},{5,6},{6,7},{8,9},{9,10},{10,11},{12,13},{... | collective-permute-start | bytes 589832 | tf_op jit(solution)/shard_map/ppermute | solution.py:224
  20.5 1.3 %collective-permute-start.2 = (f32[24,16,128]{2,0,1:T(8,128)S(1)}, f32[24,16,128]{2,0,1:T(8,128)S(1)}, u32[]{:S(2)}, u32[]{:S(2)}) collective-permute-start(f32[24,16,128]{2,0,1:T(8,128)S(1)} %pad_maximum_fusion), channel_id=1, source_target_pairs={{1,0},{2,1},{3,2},{5,4},{6,5},{7,6},{9,8},{10,9},{11,10},{13,12},{... | collective-permute-start | bytes 589832 | tf_op jit(solution)/shard_map/ppermute | solution.py:225
  21.8 1.1 copy.36
  23.0 1.1 copy.37
  24.1 0.0 collective-permute-done.3
  24.1 2.9 %collective-permute-done.2 = f32[24,16,128]{2,0,1:T(8,128)S(1)} collective-permute-done((f32[24,16,128]{2,0,1:T(8,128)S(1)}, f32[24,16,128]{2,0,1:T(8,128)S(1)}, u32[]{:S(2)}, u32[]{:S(2)}) %collective-permute-start.2) | collective-permute-done | bytes 196640 | tf_op jit(solution)/shard_map/ppermute | solution.py:225
  27.0 0.7 copy.38
  27.7 0.0 copy-start
  27.7 24.2 %krylov.1 = (bf16[16,160,2048]{2,1,0:T(8,128)(2,1)}, f32[64,64]{1,0:T(8,128)}) custom-call(f32[16,2,8,2048]{3,2,1,0:T(8,128)} %bitcast.24, f32[4,2,8,2048]{3,2,1,0:T(8,128)} %bitcast.27, f32[4,2,8,2048]{3,2,1,0:T(8,128)} %bitcast.26, f32[24,2,8,128]{3,2,1,0:T(8,128)} %bitcast.28, f32[64,160]{1,0:T(8,128)} %constant.4.clone.pick), custom_call_target="tpu_custom_call" | custom-call | tf_op jit(solution)/shard_map/krylov/pallas_call | solution.py:232
  51.9 0.9 select_reduce_fusion
  52.8 0.9 fusion.14
  53.6 0.1 fusion.8
  53.7 0.1 fusion.9
  53.8 22.6 %all_to_all.10 = f32[32,16,128]{2,1,0:T(8,128)S(1)} all-to-all(f32[32,16,128]{2,1,0:T(8,128)S(1)} %broadcast_in_dim.45), channel_id=1, replica_groups=mesh['z'=16,'y'=4,'core'=2,'x'=4] {'y','core','x'}, dimensions={0} | all-to-all | bytes 524288 | tf_op jit(solution)/shard_map/all_to_all | solution.py:258
  76.4 0.7 broadcast_in_dim.46
  77.1 9.7 %all-to-all-start.1 = ((f32[16,16,128]{2,1,0:T(8,128)}), f32[16,16,128]{2,1,0:T(8,128)S(1)}, u32[]{:S(2)}, u32[]{:S(2)}) async-start(f32[16,16,128]{2,1,0:T(8,128)} %broadcast_in_dim.46), calls=%async_computation.1 | async-start | bytes 262144 | tf_op jit(solution)/shard_map/all_to_all | solution.py:258
  86.8 0.0 copy-done
  86.8 0.7 copy.29.shifts
  87.5 11.4 %all-to-all-done.1 = f32[16,16,128]{2,1,0:T(8,128)S(1)} async-done(((f32[16,16,128]{2,1,0:T(8,128)}), f32[16,16,128]{2,1,0:T(8,128)S(1)}, u32[]{:S(2)}, u32[]{:S(2)}) %all-to-all-start.1) | async-done | bytes 131104 | tf_op jit(solution)/shard_map/all_to_all | solution.py:258
  99.0 0.1 fusion.15
  99.1 0.2 fusion.3
  99.2 0.1 fusion.1
  99.3 0.1 copy.27
  99.4 0.1 copy.28
  99.5 0.7 fusion.gram
  100.2 19.8 %solve.1 = f32[16,12,2048]{2,1,0:T(8,128)} custom-call(f32[6,2]{1,0:T(8,128)} %copy.29.shifts, f32[64,128]{1,0:T(8,128)} %fusion.gram, f32[64,48]{1,0:T(8,128)} %constant.14.clone.spread, bf16[16,160,2048]{2,1,0:T(8,128)(2,1)} %get-tuple-element.8.basis_hbm), custom_call_target="tpu_custom_call" | custom-call | tf_op jit(solution)/shard_map/solve/pallas_call | solution.py:272
  120.0 3.6 %copy.30 = f32[12,16,2048]{2,1,0:T(8,128)} copy(f32[12,16,2048]{2,0,1:T(8,128)} %bitcast.25) | data formatting | bytes 3145728 | tf_op jit(solution)/shard_map/transpose | solution.py:289
  (13 shorter events, 0.2 us)
Async XLA Ops:
  2.2 13.2 %collective-permute-start = (f32[4,16,2048]{2,0,1:T(4,128)S(1)}, f32[4,16,2048]{2,0,1:T(4,128)S(1)}, u32[]{:S(2)}, u32[]{:S(2)}) collective-permute-start(f32[4,16,2048]{2,0,1:T(4,128)S(1)} %get-tuple-element.12), channel_id=1, source_target_pairs={{0,4},{4,8},{8,12},{12,16},{16,20},{20,24},{24,28},{28,32},{32,36}... | collective-permute-start | bytes 1572872 | tf_op jit(solution)/shard_map/ppermute | solution.py:219
  6.8 10.5 %collective-permute-start.1 = (f32[4,16,2048]{2,0,1:T(4,128)S(1)}, f32[4,16,2048]{2,0,1:T(4,128)S(1)}, u32[]{:S(2)}, u32[]{:S(2)}) collective-permute-start(f32[4,16,2048]{2,0,1:T(4,128)S(1)} %get-tuple-element.11), channel_id=1, source_target_pairs={{0,508},{4,0},{8,4},{12,8},{16,12},{20,16},{24,20},{28,24},{32,28}... | collective-permute-start | bytes 1572872 | tf_op jit(solution)/shard_map/ppermute | solution.py:220
  17.3 6.7 %collective-permute-start.3 = (f32[24,16,128]{2,0,1:T(8,128)S(1)}, f32[24,16,128]{2,0,1:T(8,128)S(1)}, u32[]{:S(2)}, u32[]{:S(2)}) collective-permute-start(f32[24,16,128]{2,0,1:T(8,128)S(1)} %pad_maximum_fusion.1), channel_id=1, source_target_pairs={{0,1},{1,2},{2,3},{4,5},{5,6},{6,7},{8,9},{9,10},{10,11},{12,13},{... | collective-permute-start | bytes 589832 | tf_op jit(solution)/shard_map/ppermute | solution.py:224
  20.5 6.4 %collective-permute-start.2 = (f32[24,16,128]{2,0,1:T(8,128)S(1)}, f32[24,16,128]{2,0,1:T(8,128)S(1)}, u32[]{:S(2)}, u32[]{:S(2)}) collective-permute-start(f32[24,16,128]{2,0,1:T(8,128)S(1)} %pad_maximum_fusion), channel_id=1, source_target_pairs={{1,0},{2,1},{3,2},{5,4},{6,5},{7,6},{9,8},{10,9},{11,10},{13,12},{... | collective-permute-start | bytes 589832 | tf_op jit(solution)/shard_map/ppermute | solution.py:225
  27.7 59.1 %copy-start = (f32[6,2]{0,1:T(2,128)S(1)}, f32[6,2]{0,1:T(2,128)}, u32[]{:S(2)}) copy-start(f32[6,2]{0,1:T(2,128)} %param.9) | copy-start | bytes 148
  77.1 21.9 %all-to-all-start.1 = ((f32[16,16,128]{2,1,0:T(8,128)}), f32[16,16,128]{2,1,0:T(8,128)S(1)}, u32[]{:S(2)}, u32[]{:S(2)}) async-start(f32[16,16,128]{2,1,0:T(8,128)} %broadcast_in_dim.46), calls=%async_computation.1 | async-start | bytes 262144 | tf_op jit(solution)/shard_map/all_to_all | solution.py:258

commit v2 on v1

v2 whole, which is shorter than its diff:
```python
import jax
import jax.numpy as jnp
import numpy as np
from jax import lax
from jax.experimental import pallas as pl
from jax.experimental.pallas import tpu as pltpu
from jax.sharding import Mesh
from jax.sharding import PartitionSpec as P

S = 4
THETA = (-8.0, -2.0, -14.0, -5.0)
SCALE = 8.0
CH = 12
HALO = 4
LANE = 128
HIGH = lax.Precision.HIGHEST
F32 = jnp.float32
BF16 = jnp.bfloat16
HI_AT = (0, 16, 32, 48, 128)
LO_AT = (64, 80, 96, 112, 144)
ROWS = 160


def selection():
    pick = np.zeros((128, ROWS), np.float32)
    for k in range(S + 1):
        for c in range(CH):
            i = k * CH + c
            at = i if i < 30 else i + 2
            pick[at, HI_AT[k] + c] = 1.0
            pick[at, LO_AT[k] + c] = 1.0
    return pick


def expansion():
    spread = np.zeros((64, 48), np.float32)
    for k in range(S):
        for c in range(CH):
            spread[k * 16 + c, k * CH + c] = 1.0
    return spread


def split(value):
    high = value.astype(BF16)
    return high, (value - high.astype(F32)).astype(BF16)


def coefficients(coef, at, field):
    shape = (8, field.shape[-1])
    spread = jnp.broadcast_to(field[1, 4:5, :], shape) * (1.0 / SCALE)
    drift_x = jnp.broadcast_to(field[1, 5:6, :], shape) * (0.5 / SCALE)
    drift_y = jnp.broadcast_to(field[1, 6:7, :], shape) * (0.5 / SCALE)
    coef[at, 0] = spread + drift_x
    coef[at, 1] = spread - drift_x
    coef[at, 2] = spread + drift_y
    coef[at, 3] = spread - drift_y
    coef[at, 4] = -4.0 * spread


def newton_row(coef, at, k, center, after, before):
    wide = center.shape[-1]
    return (
        coef[at, 0][None] * after
        + coef[at, 1][None] * before
        + coef[at, 2][None] * pltpu.roll(center, wide - 1, 2)
        + coef[at, 3][None] * pltpu.roll(center, 1, 2)
        + (coef[at, 4] - THETA[k] / SCALE)[None] * center
    )


def keep(pieces, at, k, value):
    cols = pieces.shape[-1]
    hi, lo = split(value[:, :, :cols].reshape(16, cols))
    pieces[at, HI_AT[k] : HI_AT[k] + 16, :] = hi
    pieces[at, LO_AT[k] : LO_AT[k] + 16, :] = lo


def add_gram(acc, rows):
    acc[...] += lax.dot_general(rows, rows, (((1,), (1,)), ((), ())), preferred_element_type=F32)


def middle_kernel(own, side, basis, first, second, third, acc, v1, v2, v3, coef, pieces, sems):
    tile_rows = own.shape[0]
    levels = (None, v1, v2, v3)
    acc[...] = jnp.zeros_like(acc)
    copies = []

    def start(source, target):
        copy = pltpu.make_async_copy(source, target, sems.at[len(copies)])
        copy.start()
        copies.append(copy)

    def get(k, r):
        if k:
            return levels[k][r]
        return jnp.concatenate([own[r], side[r]], axis=2)

    for front in range(1, tile_rows + 1):
        if front < tile_rows - 1:
            coefficients(coef, front, get(0, front))
        for k in range(S):
            r = front - k
            if k < r < tile_rows - 1 - k:
                value = newton_row(coef, r, k, get(k, r), get(k, r + 1), get(k, r - 1))
                if k < S - 1:
                    levels[k + 1][r] = value
                    group, at = (first, second, third)[k], export_at(k + 1, r, tile_rows)
                    if at is not None:
                        start(levels[k + 1].at[r], group.at[at])
                if HALO <= r < tile_rows - HALO:
                    keep(pieces, r - HALO, k + 1, value)
                    if k == 0:
                        keep(pieces, r - HALO, 0, get(0, r))
        r = front - S
        if HALO <= r < tile_rows - HALO:
            add_gram(acc, pieces[r - HALO])
            start(pieces.at[r - HALO, 0:128, :], basis.at[r - HALO])
    for copy in copies:
        copy.wait()


def export_at(k, r, tile_rows):
    low = {1: (1, 2, 3), 2: (2, 3), 3: (3, 4)}[k]
    rows = low + tuple(tile_rows - 1 - i for i in reversed(low))
    return rows.index(r) if r in rows else None


def edge_kernel(
    own, side, low, high, first, second, third, middle, pick, basis, payload, v1, v2, v3, coef, pieces, acc, sems
):
    tile_rows = own.shape[0]
    levels = (None, v1, v2, v3)
    exports = (None, first, second, third)
    acc[...] = middle[...]
    copies = []

    def get(k, r):
        if k:
            at = export_at(k, r, tile_rows)
            return levels[k][r + HALO] if at is None else exports[k][at]
        if r < 0:
            return low[r + HALO]
        if r >= tile_rows:
            return high[r - tile_rows]
        return jnp.concatenate([own[r], side[r]], axis=2)

    def finish(at):
        add_gram(acc, pieces[at])
        copy = pltpu.make_async_copy(pieces.at[at, 0:128, :], basis.at[at], sems.at[at])
        copy.start()
        copies.append(copy)

    ready = []
    for far in (False, True):
        def place(i):
            return tile_rows - 1 - i if far else i

        def slot(i):
            return i + HALO if far else i

        for i in range(1 - HALO, HALO):
            coefficients(coef, place(i) + HALO, get(0, place(i)))
        for k in range(S):
            for i in range(k + 1 - HALO, k + 1):
                r = place(i)
                value = newton_row(coef, r + HALO, k, get(k, r), get(k, r + 1), get(k, r - 1))
                if k < S - 1:
                    levels[k + 1][r + HALO] = value
                if i >= 0:
                    keep(pieces, slot(i), k + 1, value)
                if k == S - 1:
                    ready.append(slot(i))
                if ready and (far or k == S - 1) and i % 2 == 1:
                    finish(ready.pop(0))
            for i in range(k + 1, HALO):
                if k < S - 1:
                    keep(pieces, slot(i), k + 1, get(k + 1, place(i)))
            if k == 0:
                for i in range(HALO):
                    keep(pieces, slot(i), 0, get(0, place(i)))
    for at in ready:
        finish(at)

    half = jnp.dot(pick[0:64, :], acc[...], precision=HIGH, preferred_element_type=F32)
    gram = lax.dot_general(half, pick[...], (((1,), (1,)), ((), ())), precision=HIGH, preferred_element_type=F32)
    row = lax.broadcasted_iota(jnp.int32, (32, 128), 0)
    column = lax.broadcasted_iota(jnp.int32, (32, 128), 1)
    one, two = gram[0:32], gram[32:64]
    cross = pltpu.roll(one, 96, 1)
    shifted = pltpu.roll(one, 32, 1)
    diagonal = jnp.sum(jnp.where(column == row + 32, two, 0.0), axis=1, keepdims=True)
    packed = jnp.where(row + 32 >= column, shifted, two)
    packed = jnp.where(column == 63, jnp.broadcast_to(diagonal, (32, 128)), packed)
    whole = jnp.where(column < 32, cross, packed)
    whole = jnp.where(column < 64, whole, 0.0)
    folded = whole[0:16] + pltpu.roll(whole[16:32], 64, 1)
    payload[...] = jnp.broadcast_to(folded[None], payload.shape)
    for copy in copies:
        copy.wait()


def lane(shape):
    return lax.broadcasted_iota(jnp.int32, shape, len(shape) - 1)


def unpack(parts):
    total = parts[0]
    for i in range(1, parts.shape[0]):
        total = total + parts[i]
    row = lax.broadcasted_iota(jnp.int32, (32, 128), 0)
    column = lax.broadcasted_iota(jnp.int32, (32, 128), 1)
    whole = jnp.concatenate([total, pltpu.roll(total, 64, 1)], axis=0)
    whole = jnp.where(column < 64, whole, 0.0)
    flipped = jnp.concatenate([whole, jnp.zeros((96, 128), F32)], axis=0).T
    packed = pltpu.roll(whole, 96, 1)
    turned = flipped[32:64]
    diagonal = jnp.broadcast_to(whole[:, 63:64], (32, 128))
    first = jnp.where(row >= column, packed, turned)
    second = jnp.where(row < column, packed, turned)
    second = jnp.where(row == column, diagonal, second)
    left = column < 32
    top = jnp.where(left, first, pltpu.roll(whole, 32, 1))
    bottom = jnp.where(left, flipped[0:32], pltpu.roll(second, 32, 1))
    gram = jnp.concatenate([top, bottom], axis=0)
    gram = jnp.where(lane((64, 128)) < 30, gram, pltpu.roll(gram, 126, 1))
    return jnp.where(lax.broadcasted_iota(jnp.int32, (64, 128), 0) < 30, gram, pltpu.roll(gram, 62, 0))


def normal_systems(g, shifts):
    lanes = lane((48, 128))
    rows_id = lax.broadcasted_iota(jnp.int32, (48, 128), 0)
    theta_col = jnp.zeros((48, 128), F32)
    theta_row = jnp.zeros((48, 128), F32)
    for k in range(S):
        theta_row = jnp.where((rows_id >= 12 * k) & (rows_id < 12 * k + 12), THETA[k], theta_row)
        theta_col = jnp.where((lanes >= 12 * k) & (lanes < 12 * k + 12), THETA[k], theta_col)
    g0 = g[0:48]
    gd = pltpu.roll(g, 64 - 12, 0)[0:48]
    gr = pltpu.roll(g0, 128 - 12, 1)
    grd = pltpu.roll(gd, 128 - 12, 1)
    inside = lanes < 48
    at_rhs = lanes == 48
    systems = []
    for j in range(CH // 2):
        a = shifts[0, j]
        b = shifts[1, j]
        alpha_i = theta_row - a
        alpha_l = theta_col - a
        real = (alpha_i * alpha_l + b * b) * g0 + SCALE * (alpha_i * gr + alpha_l * gd) + SCALE * SCALE * grd
        imag = b * ((alpha_l - alpha_i) * g0 + SCALE * (gr - gd))
        g1 = pltpu.roll(g0, 48 - 2 * j, 1)
        g2 = pltpu.roll(g0, 47 - 2 * j, 1)
        gd1 = pltpu.roll(gd, 48 - 2 * j, 1)
        gd2 = pltpu.roll(gd, 47 - 2 * j, 1)
        rhs_real = alpha_i * g1 - b * g2 + SCALE * gd1
        rhs_imag = alpha_i * g2 + b * g1 + SCALE * gd2
        real = jnp.where(inside, real, jnp.where(at_rhs, rhs_real, 0.0))
        imag = jnp.where(inside, imag, jnp.where(at_rhs, rhs_imag, 0.0))
        system = real + pltpu.roll(imag, 64, 1)
        systems.append([system[8 * i : 8 * i + 8] for i in range(6)])
    return systems


def column_of(block, at):
    return jnp.broadcast_to(block[:, at : at + 1], (8, 128))


def eliminate(systems):
    flip = jnp.where(lane((1, 128)) < 64, -1.0, 1.0)
    rows_id = lax.broadcasted_iota(jnp.int32, (8, 128), 0)
    for k in range(0, 48, 2):
        at, p = k // 8, k % 8
        for blocks in systems:
            pivot = blocks[at]
            row0, row1 = pivot[p : p + 1], pivot[p + 1 : p + 2]
            turn0 = pltpu.roll(row0, 64, 1) * flip
            turn1 = pltpu.roll(row1, 64, 1) * flip
            columns = [
                [column_of(b, c) for c in (k, 64 + k, k + 1, 65 + k)] for b in blocks
            ]
            c0r, _, c1r, c1i = columns[at]
            a, zr, zi, d = c0r[p : p + 1], c1r[p : p + 1], c1i[p : p + 1], c1r[p + 1 : p + 2]
            scale = 1.0 / (a * d - (zr * zr + zi * zi))
            a, zr, zi, d = a * scale, zr * scale, zi * scale, d * scale
            x0 = d * row0 - (zr * row1 + zi * turn1)
            x1 = a * row1 - (zr * row0 - zi * turn0)
            t0 = d * turn0 - (zr * turn1 - zi * row1)
            t1 = a * turn1 - (zr * turn0 + zi * row0)
            for i in range(6):
                c0r, c0i, c1r, c1i = columns[i]
                update = blocks[i] - ((c0r * x0 + c0i * t0) + (c1r * x1 + c1i * t1))
                if i == at:
                    update = jnp.where(rows_id == p, x0, jnp.where(rows_id == p + 1, x1, update))
                blocks[i] = update
    return systems


def solve_kernel(shifts, parts, spread, middle_hbm, edge_hbm, out, middle, edge, mixed, sems):
    tile_rows = middle.shape[0] + edge.shape[0]
    strips = mixed.shape[0]
    copies = [
        pltpu.make_async_copy(middle_hbm, middle, sems.at[0]),
        pltpu.make_async_copy(edge_hbm, edge, sems.at[1]),
    ]
    for copy in copies:
        copy.start()

    systems = eliminate(normal_systems(unpack(parts), shifts))
    lanes = lane((48, 128))
    mix = jnp.zeros((48, 128), F32)
    for j, blocks in enumerate(systems):
        m = jnp.concatenate(blocks, axis=0)
        mix = jnp.where(lanes == 2 * j, jnp.broadcast_to(m[:, 48:49], (48, 128)), mix)
        mix = jnp.where(lanes == 2 * j + 1, jnp.broadcast_to(m[:, 112:113], (48, 128)), mix)
    mix = jnp.dot(spread[...], mix, precision=HIGH, preferred_element_type=F32)
    mix_hi, mix_lo = split(mix)
    weights = mix_hi.astype(F32) + pltpu.roll(mix_lo.astype(F32), 16, 1)
    weights = jnp.concatenate([weights, weights], axis=0).T[0:32].astype(BF16)

    for copy in copies:
        copy.wait()

    def combine(pieces, r):
        both = jnp.dot(weights, pieces, preferred_element_type=F32)
        both = both[0:16] + both[16:32]
        for j in range(strips):
            mixed.at[j][pl.ds(r, CH, stride=tile_rows), :] = both[0:CH, j * LANE : (j + 1) * LANE]

    for i in range(tile_rows - 2 * HALO):
        combine(middle[i], i + HALO)
    for i in range(HALO):
        combine(edge[i], i)
        combine(edge[i + HALO], tile_rows - 1 - i)
    copies = [
        pltpu.make_async_copy(mixed.at[j], out.at[:, j * LANE : (j + 1) * LANE], sems.at[2 + j]) for j in range(strips)
    ]
    for copy in copies:
        copy.start()
    for copy in copies:
        copy.wait()


def per_device(right_side, diffusion, drift_field, shifts):
    tile_rows, tile_cols = right_side.shape[1:]
    wide, mid_rows, depth = tile_cols + LANE, tile_rows - 2 * HALO, tile_rows + 2 * HALO
    raw = (right_side, diffusion[None], drift_field, jnp.zeros((1, tile_rows, tile_cols), F32))
    gy = lax.axis_size("x")
    from_left = lax.ppermute(
        jnp.concatenate([f[:, :, -LANE:] for f in raw]), "x", [(i, i + 1) for i in range(gy - 1)]
    )
    from_right = lax.ppermute(
        jnp.concatenate([f[:, :, :LANE] for f in raw]), "x", [(i + 1, i) for i in range(gy - 1)]
    )
    side = jnp.where(lax.broadcasted_iota(jnp.int32, from_left.shape, 2) < LANE // 2, from_right, from_left)
    side = side.transpose(1, 0, 2)
    fields = jnp.concatenate(raw, axis=0).transpose(1, 0, 2)
    gx = ("z", "y", "core")
    count = lax.axis_size(gx)
    low = lax.ppermute(
        jnp.concatenate([fields[-HALO:], side[-HALO:]], axis=2), gx, [(i, (i + 1) % count) for i in range(count)]
    )
    high = lax.ppermute(
        jnp.concatenate([fields[:HALO], side[:HALO]], axis=2), gx, [(i, (i - 1) % count) for i in range(count)]
    )

    def halves(x):
        return x.reshape(x.shape[0], 2, 8, x.shape[2])

    def rows_of(n, width=wide):
        return (n, 2, 8, width)

    fields, side, low, high = halves(fields), halves(side), halves(low), halves(high)
    anywhere = pl.BlockSpec(memory_space=pl.ANY)
    vmem = pl.BlockSpec(memory_space=pltpu.VMEM)
    params = pltpu.CompilerParams(vmem_limit_bytes=60 * 2**20)
    middle, first, second, third, partial = pl.pallas_call(
        middle_kernel,
        out_shape=(
            jax.ShapeDtypeStruct((mid_rows, 128, tile_cols), BF16),
            jax.ShapeDtypeStruct(rows_of(6), F32),
            jax.ShapeDtypeStruct(rows_of(4), F32),
            jax.ShapeDtypeStruct(rows_of(4), F32),
            jax.ShapeDtypeStruct((ROWS, ROWS), F32),
        ),
        in_specs=[vmem, vmem],
        out_specs=(anywhere, anywhere, anywhere, anywhere, vmem),
        scratch_shapes=[
            *[pltpu.VMEM(rows_of(tile_rows), F32) for _ in range(3)],
            pltpu.VMEM((tile_rows, 5, 8, wide), F32),
            pltpu.VMEM((mid_rows, ROWS, tile_cols), BF16),
            pltpu.SemaphoreType.DMA((14 + mid_rows,)),
        ],
        compiler_params=params,
        cost_estimate=pl.CostEstimate(flops=10**9, bytes_accessed=20 * 10**6, transcendentals=0),
        name="middle",
    )(fields, side)
    edge, payload = pl.pallas_call(
        edge_kernel,
        out_shape=(
            jax.ShapeDtypeStruct((2 * HALO, 128, tile_cols), BF16),
            jax.ShapeDtypeStruct((32, 16, LANE), F32),
        ),
        in_specs=[vmem] * 9,
        out_specs=(anywhere, vmem),
        scratch_shapes=[
            *[pltpu.VMEM(rows_of(depth), F32) for _ in range(3)],
            pltpu.VMEM((depth, 5, 8, wide), F32),
            pltpu.VMEM((2 * HALO, ROWS, tile_cols), BF16),
            pltpu.VMEM((ROWS, ROWS), F32),
            pltpu.SemaphoreType.DMA((2 * HALO,)),
        ],
        compiler_params=params,
        name="edge",
    )(fields, side, low, high, first, second, third, partial, jnp.asarray(selection()))

    parts = lax.all_to_all(payload, ("y", "core", "x"), 0, 0, tiled=True)
    total = jnp.sum(parts, axis=0)
    parts = lax.all_to_all(
        jnp.broadcast_to(total[None], (lax.axis_size("z"), 16, LANE)), ("z",), 0, 0, tiled=True
    )

    out = pl.pallas_call(
        solve_kernel,
        out_shape=jax.ShapeDtypeStruct((CH * tile_rows, tile_cols), F32),
        in_specs=[pl.BlockSpec(memory_space=pltpu.SMEM), vmem, vmem, anywhere, anywhere],
        out_specs=anywhere,
        scratch_shapes=[
            pltpu.VMEM((mid_rows, 128, tile_cols), BF16),
            pltpu.VMEM((2 * HALO, 128, tile_cols), BF16),
            pltpu.VMEM((tile_cols // LANE, CH * tile_rows, LANE), F32),
            pltpu.SemaphoreType.DMA((2 + tile_cols // LANE,)),
        ],
        compiler_params=params,
        name="solve",
    )(shifts.T, parts, jnp.asarray(expansion()), middle, edge)
    return out.reshape(CH, tile_rows, tile_cols)


def solution(mesh):
    fine = Mesh(mesh.devices.reshape(16, 4, 2, 4), ("z", "y", "core", "x"))
    gx = ("z", "y", "core")
    in_specs = (P(None, gx, "x"), P(gx, "x"), P(None, gx, "x"), P())
    return jax.shard_map(
        per_device, mesh=fine, in_specs=in_specs, out_specs=P(None, gx, "x"), check_vma=False
    )
```

time: 125 us -> 96.9 us (0.78)
  blocking collectives: 22.6 us -> 41.8 us
  Pallas kernels: 44 us -> 26.8 us
  waiting for transfers between devices: 16.1 us -> 2.28 us
  starting transfers between devices: 24.8 us -> 14.4 us
  local copies, waits for them, and re-layouts: 11.1 us -> 7.7 us
  other arithmetic: 4.94 us -> 2.3 us
    all_to_all x1 -> x2, blocking collectives: 22.6 us -> 41.8 us  [the longest x1 22.1 us: per_device(): lax.all_to_all(jnp.broadcast_to(total[None], (lax.axis_size('z'), 16, LAN...]
    pallas_call x2 -> x3, Pallas kernels: 44 us -> 26.8 us  [the longest x1 11.1 us: per_device(): pl.pallas_call(solve_kernel, out_shape=jax.ShapeDtypeStruct((CH * tile_ro...]
    all_to_all x1 -> x0, waiting for transfers between devices: 11.4 us -> none  [per_device(): lax.all_to_all(jnp.broadcast_to(payload[None], (members, 16, LANE)), axes...]
    all_to_all x1 -> x0, starting transfers between devices: 9.72 us -> none  [per_device(): lax.all_to_all(jnp.broadcast_to(payload[None], (members, 16, LANE)), axes...]
    transpose x3 -> x2, local copies, waits for them, and re-layouts: 6.27 us -> 3.27 us  [the longest x1 2.58 us: per_device(): fields = jnp.concatenate(raw, axis=0).transpose(1, 0, 2)]
    ppermute x4, waiting for transfers between devices: 4.7 us -> 2.28 us  [the longest x1 2.27 us: per_device(): lax.ppermute(jnp.concatenate([f[:, :, :LANE] for f in raw]), 'x', [(i + 1...]
    slice x6 -> x5, local copies, waits for them, and re-layouts: 0.42 us -> 2.65 us  [the longest x3 2.43 us: per_device(): f[:, :, -LANE:]]
  transfers between devices with their start and end apart: 5 -> 4, of which waited for: 3 -> 1; matrix products, arithmetic and copies ran while one was open for 4% -> 7% of each run, Pallas kernels for 0% -> 8%
where the time goes in v2:
time: 96.9 us; the launch traced here: 95.6 us
  blocking collectives  41.8 us (43%)
  Pallas kernels  26.8 us (28%)
  starting transfers between devices  14.4 us (15%)
  local copies, waits for them, and re-layouts  7.7 us (8%)
  other arithmetic  2.3 us (2%)
  waiting for transfers between devices  2.28 us (2%)
    all_to_all x1, blocking collectives, per_device(): lax.all_to_all(jnp.broadcast_to(total[None], (lax.axis_size('z'), 16, LAN...  22.1 us
    all_to_all x1, blocking collectives, per_device(): parts = lax.all_to_all(payload, ('y', 'core', 'x'), 0, 0, tiled=True)  19.8 us
    pallas_call x1, Pallas kernels, per_device(): pl.pallas_call(solve_kernel, out_shape=jax.ShapeDtypeStruct((CH * tile_ro...  11.1 us
    pallas_call x1, Pallas kernels, per_device(): pl.pallas_call(edge_kernel, out_shape=(jax.ShapeDtypeStruct((2 * HALO, 12...  7.93 us
    pallas_call x1, Pallas kernels, per_device(): pl.pallas_call(middle_kernel, out_shape=(jax.ShapeDtypeStruct((mid_rows,...  7.73 us
    ppermute x1, starting transfers between devices, per_device(): lax.ppermute(jnp.concatenate([fields[-HALO:], side[-HALO:]], axis=2), gx,...  5.19 us
    ppermute x1, starting transfers between devices, per_device(): lax.ppermute(jnp.concatenate([fields[:HALO], side[:HALO]], axis=2), gx, [...  3.98 us
    ppermute x1, starting transfers between devices, per_device(): lax.ppermute(jnp.concatenate([f[:, :, -LANE:] for f in raw]), 'x', [(i, i...  3.94 us
  transfers between devices with their start and end apart: 4, of which 1 were waited for; matrix products, arithmetic and copies ran while one was open for 7% of the time, Pallas kernels for 8%

profile of v2, /device:TPU:1, one launch (start us, length us, event | category | flops | bytes accessed | tf_op | source)
XLA Modules:
  0.0 95.6 jit_solution(14193233301231991855)
XLA Ops:
  0.0 0.7 fusion.4
  0.7 0.8 fusion.2
  1.5 1.0 fusion.1
  2.4 0.1 pad.15.clone
  2.5 0.1 maximum_maximum_fusion.1
  2.6 3.9 %collective-permute-start.1 = (f32[16,16,128]{2,1,0:T(8,128)S(1)}, f32[16,16,128]{2,1,0:T(8,128)S(1)}, u32[]{:S(2)}, u32[]{:S(2)}) collective-permute-start(f32[16,16,128]{2,1,0:T(8,128)S(1)} %get-tuple-element.29), channel_id=1, source_target_pairs={{0,1},{1,2},{2,3},{4,5},{5,6},{6,7},{8,9},{9,10},{10,11},{12,13},{... | collective-permute-start | bytes 393224 | tf_op jit(solution)/shard_map/ppermute | solution.py:348
  6.6 1.3 %collective-permute-start = (f32[16,16,128]{2,1,0:T(8,128)S(1)}, f32[16,16,128]{2,1,0:T(8,128)S(1)}, u32[]{:S(2)}, u32[]{:S(2)}) collective-permute-start(f32[16,16,128]{2,1,0:T(8,128)S(1)} %get-tuple-element.30), channel_id=1, source_target_pairs={{1,0},{2,1},{3,2},{5,4},{6,5},{7,6},{9,8},{10,9},{11,10},{13,12},{... | collective-permute-start | bytes 393224 | tf_op jit(solution)/shard_map/ppermute | solution.py:351
  7.9 1.9 %maximum_bitcast_fusion = f32[16,16,2048]{2,0,1:T(8,128)S(1)} fusion(f32[2,16,2048]{2,1,0:T(8,128)} %param.8, f32[1,16,2048]{2,1,0:T(8,128)} %bitcast.28, f32[12,16,2048]{2,1,0:T(8,128)} %param.6, f32[16]{0:T(128)S(1)} %pad.15.clone), kind=kLoop, calls=%fused_computation | loop fusion | flops 1572864 | bytes 4063296 | tf_op jit(solution)/shard_map/transpose | solution.py:356
  9.8 0.2 fusion
  10.0 0.0 collective-permute-done.1
  10.0 2.3 %collective-permute-done = f32[16,16,128]{2,1,0:T(8,128)S(1)} collective-permute-done((f32[16,16,128]{2,1,0:T(8,128)S(1)}, f32[16,16,128]{2,1,0:T(8,128)S(1)}, u32[]{:S(2)}, u32[]{:S(2)}) %collective-permute-start) | collective-permute-done | bytes 131104 | tf_op jit(solution)/shard_map/ppermute | solution.py:351
  12.3 0.1 pad_maximum_fusion
  12.4 5.2 %collective-permute-start.2 = (f32[4,16,2176]{2,0,1:T(4,128)S(1)}, f32[4,16,2176]{2,0,1:T(4,128)S(1)}, u32[]{:S(2)}, u32[]{:S(2)}) collective-permute-start(f32[4,16,2176]{2,0,1:T(4,128)S(1)} %pad_maximum_fusion), channel_id=1, source_target_pairs={{0,4},{4,8},{8,12},{12,16},{16,20},{20,24},{24,28},{28,32},{32,36}... | collective-permute-start | bytes 1671176 | tf_op jit(solution)/shard_map/ppermute | solution.py:359
  17.7 0.1 pad_maximum_fusion.1
  17.8 4.0 %collective-permute-start.3 = (f32[4,16,2176]{2,0,1:T(4,128)S(1)}, f32[4,16,2176]{2,0,1:T(4,128)S(1)}, u32[]{:S(2)}, u32[]{:S(2)}) collective-permute-start(f32[4,16,2176]{2,0,1:T(4,128)S(1)} %pad_maximum_fusion.1), channel_id=1, source_target_pairs={{0,508},{4,0},{8,4},{12,8},{16,12},{20,16},{24,20},{28,24},{32,28}... | collective-permute-start | bytes 1671176 | tf_op jit(solution)/shard_map/ppermute | solution.py:362
  21.8 2.6 %copy.15 = f32[16,16,2048]{2,1,0:T(8,128)} copy(f32[16,16,2048]{2,0,1:T(8,128)S(1)} %maximum_bitcast_fusion) | data formatting | bytes 4194304 | tf_op jit(solution)/shard_map/transpose | solution.py:356
  24.4 0.7 copy.18
  25.0 7.7 %middle.1 = (bf16[8,128,2048]{2,1,0:T(8,128)(2,1)}, f32[6,2,8,2176]{3,2,1,0:T(8,128)}, f32[4,2,8,2176]{3,2,1,0:T(8,128)}, f32[4,2,8,2176]{3,2,1,0:T(8,128)}, f32[160,160]{1,0:T(8,128)}) custom-call(f32[16,2,8,2048]{3,2,1,0:T(8,128)} %bitcast.21, f32[16,2,8,128]{3,2,1,0:T(8,128)} %bitcast.25), custom_call_target="tpu_custom_call" | custom-call | flops 1000000000 | bytes 20000000 | tf_op jit(solution)/shard_map/middle/pallas_call | solution.py:376
  32.8 0.0 collective-permute-done.2
  32.8 0.8 copy.17
  33.6 0.0 collective-permute-done.3
  33.7 0.8 copy.16
  34.5 7.9 %edge.1 = (bf16[8,128,2048]{2,1,0:T(8,128)(2,1)}, f32[32,16,128]{2,1,0:T(8,128)}) custom-call(f32[16,2,8,2048]{3,2,1,0:T(8,128)} %bitcast.22, f32[16,2,8,128]{3,2,1,0:T(8,128)} %bitcast.26, f32[4,2,8,2176]{3,2,1,0:T(8,128)} %bitcast.23, f32[4,2,8,2176]{3,2,1,0:T(8,128)} %bitcast.24, f32[6,2,8,2176]{3,2,1,0:T(8,128)} %get-tuple-element.12.first, ...), custom_call_target="tpu_custom_call" | custom-call | tf_op jit(solution)/shard_map/edge/pallas_call | solution.py:397
  42.4 19.8 %all_to_all.10 = f32[32,16,128]{2,1,0:T(8,128)S(1)} all-to-all(f32[32,16,128]{2,1,0:T(8,128)} %get-tuple-element.16), channel_id=1, replica_groups=mesh['z'=16,'y'=4,'core'=2,'x'=4] {'y','core','x'}, dimensions={0} | all-to-all | bytes 524288 | tf_op jit(solution)/shard_map/all_to_all | solution.py:416
  62.3 22.1 %all_to_all.11.parts = f32[16,16,128]{2,1,0:T(8,128)} all-to-all(f32[16,16,128]{2,1,0:T(8,128)S(1)} %broadcast_in_dim.14), channel_id=1, replica_groups=mesh['z'=16,'y'=4,'core'=2,'x'=4] {'z'}, dimensions={0} | all-to-all | bytes 262144 | tf_op jit(solution)/shard_map/all_to_all | solution.py:418
  84.3 11.1 %solve.1 = f32[192,2048]{1,0:T(8,128)} custom-call(f32[2,6]{1,0:T(2,128)} %bitcast.29, f32[16,16,128]{2,1,0:T(8,128)} %all_to_all.11.parts, f32[64,48]{1,0:T(8,128)} %constant.3.clone.spread, bf16[8,128,2048]{2,1,0:T(8,128)(2,1)} %get-tuple-element.17.middle_hbm, bf16[8,128,2048]{2,1,0:T(8,128)(2,1)} %get-tuple-element.18.edge_hbm), custom_call_target="tpu_custom_call" | custom-call | tf_op jit(solution)/shard_map/solve/pallas_call | solution.py:422
  (5 shorter events, 0.1 us)
Async XLA Ops:
  2.6 7.4 %collective-permute-start.1 = (f32[16,16,128]{2,1,0:T(8,128)S(1)}, f32[16,16,128]{2,1,0:T(8,128)S(1)}, u32[]{:S(2)}, u32[]{:S(2)}) collective-permute-start(f32[16,16,128]{2,1,0:T(8,128)S(1)} %get-tuple-element.29), channel_id=1, source_target_pairs={{0,1},{1,2},{2,3},{4,5},{5,6},{6,7},{8,9},{9,10},{10,11},{12,13},{... | collective-permute-start | bytes 393224 | tf_op jit(solution)/shard_map/ppermute | solution.py:348
  6.6 5.7 %collective-permute-start = (f32[16,16,128]{2,1,0:T(8,128)S(1)}, f32[16,16,128]{2,1,0:T(8,128)S(1)}, u32[]{:S(2)}, u32[]{:S(2)}) collective-permute-start(f32[16,16,128]{2,1,0:T(8,128)S(1)} %get-tuple-element.30), channel_id=1, source_target_pairs={{1,0},{2,1},{3,2},{5,4},{6,5},{7,6},{9,8},{10,9},{11,10},{13,12},{... | collective-permute-start | bytes 393224 | tf_op jit(solution)/shard_map/ppermute | solution.py:351
  12.4 20.3 %collective-permute-start.2 = (f32[4,16,2176]{2,0,1:T(4,128)S(1)}, f32[4,16,2176]{2,0,1:T(4,128)S(1)}, u32[]{:S(2)}, u32[]{:S(2)}) collective-permute-start(f32[4,16,2176]{2,0,1:T(4,128)S(1)} %pad_maximum_fusion), channel_id=1, source_target_pairs={{0,4},{4,8},{8,12},{12,16},{16,20},{20,24},{24,28},{28,32},{32,36}... | collective-permute-start | bytes 1671176 | tf_op jit(solution)/shard_map/ppermute | solution.py:359
  17.8 15.9 %collective-permute-start.3 = (f32[4,16,2176]{2,0,1:T(4,128)S(1)}, f32[4,16,2176]{2,0,1:T(4,128)S(1)}, u32[]{:S(2)}, u32[]{:S(2)}) collective-permute-start(f32[4,16,2176]{2,0,1:T(4,128)S(1)} %pad_maximum_fusion.1), channel_id=1, source_target_pairs={{0,508},{4,0},{8,4},{12,8},{16,12},{20,16},{24,20},{28,24},{32,28}... | collective-permute-start | bytes 1671176 | tf_op jit(solution)/shard_map/ppermute | solution.py:362

commit v3 on v2

--- a/solution.py
+++ b/solution.py
@@ -126,12 +126,13 @@
 
 
 def edge_kernel(
-    own, side, low, high, first, second, third, middle, pick, basis, payload, v1, v2, v3, coef, pieces, acc, sems
+    core, own, side, near, across, first, second, third, middle, pick, basis, payload, v1, v2, v3, coef, pieces, acc, sems
 ):
     tile_rows = own.shape[0]
     levels = (None, v1, v2, v3)
     exports = (None, first, second, third)
     acc[...] = middle[...]
+    even = core[0] == 0
     copies = []
 
     def get(k, r):
@@ -139,9 +140,9 @@
             at = export_at(k, r, tile_rows)
             return levels[k][r + HALO] if at is None else exports[k][at]
         if r < 0:
-            return low[r + HALO]
+            return jnp.where(even, across[r + HALO], near[r + HALO])
         if r >= tile_rows:
-            return high[r - tile_rows]
+            return jnp.where(even, near[r - tile_rows], across[r - tile_rows])
         return jnp.concatenate([own[r], side[r]], axis=2)
 
     def finish(at):
@@ -197,6 +198,50 @@
     payload[...] = jnp.broadcast_to(folded[None], payload.shape)
     for copy in copies:
         copy.wait()
+
+
+def gather_rows(right_side, diffusion, drift_field, strips, sems, at):
+    tile_rows = diffusion.shape[0]
+    first, second = CH * tile_rows, (CH + 1) * tile_rows
+    cols = pl.ds(at[1] * LANE, LANE)
+    copies = (
+        (right_side.at[:, cols], strips.at[at[0], 0:first]),
+        (diffusion.at[:, cols], strips.at[at[0], first:second]),
+        (drift_field.at[:, cols], strips.at[at[0], second : second + 2 * tile_rows]),
+    )
+    copies = [pltpu.make_async_copy(a, b, sems.at[at[0], i]) for i, (a, b) in enumerate(copies)]
+    for copy in copies:
+        copy.start()
+    return copies
+
+
+def edges_kernel(right_side, diffusion, drift_field, left, right, strips, sems):
+    tile_rows, tile_cols = diffusion.shape
+    outs = (left, right)
+    places = (0, tile_cols // LANE - 1)
+    copies = [gather_rows(right_side, diffusion, drift_field, strips, sems, (i, p)) for i, p in enumerate(places)]
+    for i in range(2):
+        strips[i, 15 * tile_rows :] = jnp.zeros((tile_rows, LANE), F32)
+        for copy in copies[i]:
+            copy.wait()
+        for r in range(tile_rows):
+            for half in range(2):
+                outs[i][r, half] = strips.at[i][pl.ds(8 * half * tile_rows + r, 8, stride=tile_rows), :]
+
+
+def fields_kernel(right_side, diffusion, drift_field, fields, strips, sems):
+    tile_rows, tile_cols = diffusion.shape
+    count = tile_cols // LANE
+    copies = [gather_rows(right_side, diffusion, drift_field, strips, sems, (i, i)) for i in range(count)]
+    for i in range(count):
+        strips[i, 15 * tile_rows :] = jnp.zeros((tile_rows, LANE), F32)
+        for copy in copies[i]:
+            copy.wait()
+        for r in range(tile_rows):
+            for half in range(2):
+                fields[r, half, :, i * LANE : (i + 1) * LANE] = strips.at[i][
+                    pl.ds(8 * half * tile_rows + r, 8, stride=tile_rows), :
+                ]
 
 
 def lane(shape):
@@ -343,36 +388,54 @@
 def per_device(right_side, diffusion, drift_field, shifts):
     tile_rows, tile_cols = right_side.shape[1:]
     wide, mid_rows, depth = tile_cols + LANE, tile_rows - 2 * HALO, tile_rows + 2 * HALO
-    raw = (right_side, diffusion[None], drift_field, jnp.zeros((1, tile_rows, tile_cols), F32))
-    gy = lax.axis_size("x")
-    from_left = lax.ppermute(
-        jnp.concatenate([f[:, :, -LANE:] for f in raw]), "x", [(i, i + 1) for i in range(gy - 1)]
-    )
-    from_right = lax.ppermute(
-        jnp.concatenate([f[:, :, :LANE] for f in raw]), "x", [(i + 1, i) for i in range(gy - 1)]
-    )
-    side = jnp.where(lax.broadcasted_iota(jnp.int32, from_left.shape, 2) < LANE // 2, from_right, from_left)
-    side = side.transpose(1, 0, 2)
-    fields = jnp.concatenate(raw, axis=0).transpose(1, 0, 2)
-    gx = ("z", "y", "core")
-    count = lax.axis_size(gx)
-    low = lax.ppermute(
-        jnp.concatenate([fields[-HALO:], side[-HALO:]], axis=2), gx, [(i, (i + 1) % count) for i in range(count)]
-    )
-    high = lax.ppermute(
-        jnp.concatenate([fields[:HALO], side[:HALO]], axis=2), gx, [(i, (i - 1) % count) for i in range(count)]
-    )
-
-    def halves(x):
-        return x.reshape(x.shape[0], 2, 8, x.shape[2])
+    anywhere = pl.BlockSpec(memory_space=pl.ANY)
+    vmem = pl.BlockSpec(memory_space=pltpu.VMEM)
+    far = pl.BlockSpec(memory_space=pltpu.HBM)
+    scalar = pl.BlockSpec(memory_space=pltpu.SMEM)
+
+    def params(mib):
+        return pltpu.CompilerParams(vmem_limit_bytes=mib * 2**20)
+
+    count = tile_cols // LANE
 
     def rows_of(n, width=wide):
         return (n, 2, 8, width)
 
-    fields, side, low, high = halves(fields), halves(side), halves(low), halves(high)
-    anywhere = pl.BlockSpec(memory_space=pl.ANY)
-    vmem = pl.BlockSpec(memory_space=pltpu.VMEM)
-    params = pltpu.CompilerParams(vmem_limit_bytes=60 * 2**20)
+    raw = (
+        right_side.reshape(CH * tile_rows, tile_cols),
+        diffusion,
+        drift_field.reshape(2 * tile_rows, tile_cols),
+    )
+    left, right = pl.pallas_call(
+        edges_kernel,
+        out_shape=[jax.ShapeDtypeStruct(rows_of(tile_rows, LANE), F32)] * 2,
+        in_specs=[anywhere] * 3,
+        scratch_shapes=[pltpu.VMEM((2, 16 * tile_rows, LANE), F32), pltpu.SemaphoreType.DMA((2, 3))],
+        compiler_params=params(60),
+        name="edges",
+    )(*raw)
+    gy = lax.axis_size("x")
+    from_left = lax.ppermute(right, "x", [(i, i + 1) for i in range(gy - 1)])
+    from_right = lax.ppermute(left, "x", [(i + 1, i) for i in range(gy - 1)])
+    side = jnp.where(lax.broadcasted_iota(jnp.int32, from_left.shape, 3) < LANE // 2, from_right, from_left)
+    fields = pl.pallas_call(
+        fields_kernel,
+        out_shape=jax.ShapeDtypeStruct(rows_of(tile_rows, tile_cols), F32),
+        in_specs=[anywhere] * 3,
+        scratch_shapes=[pltpu.VMEM((count, 16 * tile_rows, LANE), F32), pltpu.SemaphoreType.DMA((count, 3))],
+        compiler_params=params(60),
+        cost_estimate=pl.CostEstimate(flops=10**6, bytes_accessed=4 * 10**6, transcendentals=0),
+        name="fields",
+    )(*raw)
+    core = lax.axis_index("core")
+    start = jnp.concatenate([fields[:HALO], side[:HALO]], axis=3)
+    end = jnp.concatenate([fields[-HALO:], side[-HALO:]], axis=3)
+    gx = ("z", "y", "core")
+    ring = lax.axis_size(gx)
+    across = lax.ppermute(
+        jnp.where(core == 0, start, end), gx, [(i, (i + 2 * (i % 2) - 1) % ring) for i in range(ring)]
+    )
+    near = lax.ppermute(jnp.where(core == 0, end, start), "core", [(0, 1), (1, 0)])
     middle, first, second, third, partial = pl.pallas_call(
         middle_kernel,
         out_shape=(
@@ -383,14 +446,14 @@
             jax.ShapeDtypeStruct((ROWS, ROWS), F32),
         ),
         in_specs=[vmem, vmem],
-        out_specs=(anywhere, anywhere, anywhere, anywhere, vmem),
+        out_specs=(far, anywhere, anywhere, anywhere, vmem),
         scratch_shapes=[
             *[pltpu.VMEM(rows_of(tile_rows), F32) for _ in range(3)],
             pltpu.VMEM((tile_rows, 5, 8, wide), F32),
             pltpu.VMEM((mid_rows, ROWS, tile_cols), BF16),
             pltpu.SemaphoreType.DMA((14 + mid_rows,)),
         ],
-        compiler_params=params,
+        compiler_params=params(28),
         cost_estimate=pl.CostEstimate(flops=10**9, bytes_accessed=20 * 10**6, transcendentals=0),
         name="middle",
     )(fields, side)
@@ -400,8 +463,8 @@
             jax.ShapeDtypeStruct((2 * HALO, 128, tile_cols), BF16),
             jax.ShapeDtypeStruct((32, 16, LANE), F32),
         ),
-        in_specs=[vmem] * 9,
-        out_specs=(anywhere, vmem),
+        in_specs=[scalar, *[vmem] * 9],
+        out_specs=(far, vmem),
         scratch_shapes=[
             *[pltpu.VMEM(rows_of(depth), F32) for _ in range(3)],
             pltpu.VMEM((depth, 5, 8, wide), F32),
@@ -409,9 +472,9 @@
             pltpu.VMEM((ROWS, ROWS), F32),
             pltpu.SemaphoreType.DMA((2 * HALO,)),
         ],
-        compiler_params=params,
+        compiler_params=params(40),
         name="edge",
-    )(fields, side, low, high, first, second, third, partial, jnp.asarray(selection()))
+    )(core.reshape(1), fields, side, near, across, first, second, third, partial, jnp.asarray(selection()))
 
     parts = lax.all_to_all(payload, ("y", "core", "x"), 0, 0, tiled=True)
     total = jnp.sum(parts, axis=0)
@@ -422,7 +485,7 @@
     out = pl.pallas_call(
         solve_kernel,
         out_shape=jax.ShapeDtypeStruct((CH * tile_rows, tile_cols), F32),
-        in_specs=[pl.BlockSpec(memory_space=pltpu.SMEM), vmem, vmem, anywhere, anywhere],
+        in_specs=[scalar, vmem, vmem, far, far],
         out_specs=anywhere,
         scratch_shapes=[
             pltpu.VMEM((mid_rows, 128, tile_cols), BF16),
@@ -430,7 +493,7 @@
             pltpu.VMEM((tile_cols // LANE, CH * tile_rows, LANE), F32),
             pltpu.SemaphoreType.DMA((2 + tile_cols // LANE,)),
         ],
-        compiler_params=params,
+        compiler_params=params(60),
         name="solve",
     )(shifts.T, parts, jnp.asarray(expansion()), middle, edge)
     return out.reshape(CH, tile_rows, tile_cols)

time: 96.9 us -> 95.8 us (0.989)
  blocking collectives: 41.8 us -> 33.3 us
  starting transfers between devices: 14.4 us -> 22.1 us
  Pallas kernels: 26.8 us -> 33.4 us
  local copies, waits for them, and re-layouts: 7.7 us -> 5.36 us
  waiting for transfers between devices: 2.28 us -> 0.01 us
  other arithmetic: 2.3 us -> 0.15 us
    ppermute x4, starting transfers between devices: 14.4 us -> 22.1 us  [the longest x1 11.6 us: per_device(): lax.ppermute(jnp.where(core == 0, end, start), 'core', [(0, 1), (1, 0)])]
    all_to_all x1, blocking collectives: 19.8 us -> 13.2 us  [per_device(): parts = lax.all_to_all(payload, ('y', 'core', 'x'), 0, 0, tiled=True)]
    pallas_call x0 -> x2, Pallas kernels: none -> 5.25 us  [the longest x1 3.53 us: per_device(): pl.pallas_call(fields_kernel, out_shape=jax.ShapeDtypeStruct(rows_of(tile...]
    unnamed x0 -> x8, local copies, waits for them, and re-layouts: none -> 3.92 us
    transpose x2 -> x0, local copies, waits for them, and re-layouts: 3.27 us -> none  [the longest x1 2.58 us: per_device(): fields = jnp.concatenate(raw, axis=0).transpose(1, 0, 2)]
    ppermute x4, waiting for transfers between devices: 2.28 us -> 0.01 us  [the longest x1 0.01 us: per_device(): from_right = lax.ppermute(left, 'x', [(i + 1, i) for i in range(gy - 1)])]
    pallas_call x1, Pallas kernels: 7.73 us -> 9.92 us  [per_device(): pl.pallas_call(middle_kernel, out_shape=(jax.ShapeDtypeStruct((mid_rows,...]
    all_to_all x1, blocking collectives: 22.1 us -> 20.1 us  [per_device(): lax.all_to_all(jnp.broadcast_to(total[None], (lax.axis_size('z'), 16, LAN...]
  transfers between devices with their start and end apart: 4 -> 4, of which waited for: 1 -> 0; matrix products, arithmetic and copies ran while one was open for 7% -> 2% of each run, Pallas kernels for 8% -> 14%
where the time goes in v3:
time: 95.8 us; the launch traced here: 94.6 us
  Pallas kernels  33.4 us (35%)
  blocking collectives  33.3 us (35%)
  starting transfers between devices  22.1 us (23%)
  local copies, waits for them, and re-layouts  5.36 us (6%)
    all_to_all x1, blocking collectives, per_device(): lax.all_to_all(jnp.broadcast_to(total[None], (lax.axis_size('z'), 16, LAN...  20.1 us
    all_to_all x1, blocking collectives, per_device(): parts = lax.all_to_all(payload, ('y', 'core', 'x'), 0, 0, tiled=True)  13.2 us
    ppermute x1, starting transfers between devices, per_device(): lax.ppermute(jnp.where(core == 0, end, start), 'core', [(0, 1), (1, 0)])  11.6 us
    pallas_call x1, Pallas kernels, per_device(): pl.pallas_call(solve_kernel, out_shape=jax.ShapeDtypeStruct((CH * tile_ro...  11.1 us
    pallas_call x1, Pallas kernels, per_device(): pl.pallas_call(middle_kernel, out_shape=(jax.ShapeDtypeStruct((mid_rows,...  9.92 us
    pallas_call x1, Pallas kernels, per_device(): pl.pallas_call(edge_kernel, out_shape=(jax.ShapeDtypeStruct((2 * HALO, 12...  7.1 us
    ppermute x1, starting transfers between devices, per_device(): lax.ppermute(jnp.where(core == 0, start, end), gx, [(i, (i + 2 * (i % 2)...  4.7 us
    ppermute x1, starting transfers between devices, per_device(): from_left = lax.ppermute(right, 'x', [(i, i + 1) for i in range(gy - 1)])  4.57 us
  transfers between devices with their start and end apart: 4, of which 0 were waited for; matrix products, arithmetic and copies ran while one was open for 2% of the time, Pallas kernels for 14%

profile of v3, /device:TPU:1, one launch (start us, length us, event | category | flops | bytes accessed | tf_op | source)
XLA Modules:
  0.0 94.6 jit_solution(12696494379771895227)
XLA Ops:
  0.0 1.7 %edges.1 = (f32[16,2,8,128]{3,2,1,0:T(8,128)}, f32[16,2,8,128]{3,2,1,0:T(8,128)}) custom-call(f32[192,2048]{1,0:T(8,128)} %bitcast.5, f32[16,2048]{1,0:T(8,128)} %diffusion.3, f32[32,2048]{1,0:T(8,128)} %bitcast.7), custom_call_target="tpu_custom_call" | custom-call | tf_op jit(solution)/shard_map/edges/pallas_call | solution.py:409
  1.7 1.3 %collective-permute-start = (f32[16,2,8,128]{3,2,1,0:T(8,128)}, f32[16,2,8,128]{3,2,1,0:T(8,128)S(1)}, u32[]{:S(2)}, u32[]{:S(2)}) collective-permute-start(f32[16,2,8,128]{3,2,1,0:T(8,128)} %get-tuple-element.14), channel_id=1, source_target_pairs={{1,0},{2,1},{3,2},{5,4},{6,5},{7,6},{9,8},{10,9},{11,10},{13,12},{... | collective-permute-start | bytes 393224 | tf_op jit(solution)/shard_map/ppermute | solution.py:419
  3.0 4.6 %collective-permute-start.1 = (f32[16,2,8,128]{3,2,1,0:T(8,128)}, f32[16,2,8,128]{3,2,1,0:T(8,128)S(1)}, u32[]{:S(2)}, u32[]{:S(2)}) collective-permute-start(f32[16,2,8,128]{3,2,1,0:T(8,128)} %get-tuple-element.15), channel_id=1, source_target_pairs={{0,1},{1,2},{2,3},{4,5},{5,6},{6,7},{8,9},{9,10},{10,11},{12,13},{... | collective-permute-start | bytes 393224 | tf_op jit(solution)/shard_map/ppermute | solution.py:418
  7.6 3.5 %fields.1.own = f32[16,2,8,2048]{3,2,1,0:T(8,128)} custom-call(f32[192,2048]{1,0:T(8,128)} %bitcast.6, f32[16,2048]{1,0:T(8,128)} %diffusion.3, f32[32,2048]{1,0:T(8,128)} %bitcast.8), custom_call_target="tpu_custom_call" | custom-call | flops 1000000 | bytes 4000000 | tf_op jit(solution)/shard_map/fields/pallas_call | solution.py:421
  11.1 0.0 copy-start
  11.2 1.4 %fusion.2 = (f32[4,2,8,2048]{3,2,1,0:T(8,128)S(1)}, f32[4,2,8,2048]{3,2,1,0:T(8,128)S(1)}) fusion(f32[16,2,8,2048]{3,2,1,0:T(8,128)} %fields.1.own), kind=kLoop, calls=%fused_computation.6 | loop fusion | bytes 2097152 | tf_op jit(solution)/shard_map/slice | solution.py:432
  12.6 0.0 collective-permute-done
  12.6 0.0 collective-permute-done.1
  12.7 0.1 fusion
  12.8 0.0 copy-start.3
  12.8 4.7 %collective-permute-start.3 = (f32[4,2,8,2176]{3,2,1,0:T(8,128)S(1)}, f32[4,2,8,2176]{3,2,1,0:T(8,128)S(1)}, u32[]{:S(2)}, u32[]{:S(2)}) collective-permute-start(f32[4,2,8,2176]{3,2,1,0:T(8,128)S(1)} %get-tuple-element.25), channel_id=1, source_target_pairs={{0,508},{4,8},{8,4},{12,16},{16,12},{20,24},{24,20},{28,32},{32,28... | collective-permute-start | bytes 1671176 | tf_op jit(solution)/shard_map/ppermute | solution.py:435
  17.5 11.6 %collective-permute-start.2 = (f32[4,2,8,2176]{3,2,1,0:T(8,128)S(1)}, f32[4,2,8,2176]{3,2,1,0:T(8,128)S(1)}, u32[]{:S(2)}, u32[]{:S(2)}) collective-permute-start(f32[4,2,8,2176]{3,2,1,0:T(8,128)S(1)} %get-tuple-element.26), channel_id=1, source_target_pairs={{0,4},{4,0},{1,5},{5,1},{2,6},{6,2},{3,7},{7,3},{8,12},{12,8},{9,1... | collective-permute-start | bytes 1671176 | tf_op jit(solution)/shard_map/ppermute | solution.py:438
  29.0 0.0 copy-done
  29.0 9.9 %middle.1 = (bf16[8,128,2048]{2,1,0:T(8,128)(2,1)S(1)}, f32[6,2,8,2176]{3,2,1,0:T(8,128)S(1)}, f32[4,2,8,2176]{3,2,1,0:T(8,128)S(1)}, f32[4,2,8,2176]{3,2,1,0:T(8,128)S(1)}, f32[160,160]{1,0:T(8,128)S(1)}) custom-call(f32[16,2,8,2048]{3,2,1,0:T(8,128)S(1)} %copy-done, f32[16,2,8,128]{3,2,1,0:T(8,128)S(1)} %broadcast_select_fusion.side), custom_call_target="tpu_custom_call" | custom-call | flops 1000000000 | bytes 20000000 | tf_op jit(solution)/shard_map/middle/pallas_call | solution.py:439
  39.0 0.0 copy-start.1
  39.0 1.9 %copy-done.1 = bf16[8,128,2048]{2,1,0:T(8,128)(2,1)} copy-done((bf16[8,128,2048]{2,1,0:T(8,128)(2,1)}, bf16[8,128,2048]{2,1,0:T(8,128)(2,1)S(1)}, u32[]{:S(2)}) %copy-start.1) | copy-done | bytes 4194328
  40.9 0.0 collective-permute-done.3.across
  40.9 0.0 collective-permute-done.2.near
  40.9 0.0 copy-done.3
  40.9 7.1 %edge.1 = (bf16[8,128,2048]{2,1,0:T(8,128)(2,1)S(1)}, f32[32,16,128]{2,1,0:T(8,128)S(1)}) custom-call(s32[1]{0:T(128)} %bitcast.1.core, f32[16,2,8,2048]{3,2,1,0:T(8,128)S(1)} %copy-done, f32[16,2,8,128]{3,2,1,0:T(8,128)S(1)} %broadcast_select_fusion.side, f32[4,2,8,2176]{3,2,1,0:T(8,128)S(1)} %collective-permute-done.2.near, ...), custom_call_target="tpu_custom_call" | custom-call | tf_op jit(solution)/shard_map/edge/pallas_call | solution.py:460
  48.1 0.0 copy-start.2
  48.1 2.0 %copy-done.2 = bf16[8,128,2048]{2,1,0:T(8,128)(2,1)} copy-done((bf16[8,128,2048]{2,1,0:T(8,128)(2,1)}, bf16[8,128,2048]{2,1,0:T(8,128)(2,1)S(1)}, u32[]{:S(2)}) %copy-start.2) | copy-done | bytes 4194328
  50.0 13.2 %all_to_all.10 = f32[32,16,128]{2,1,0:T(8,128)S(1)} all-to-all(f32[32,16,128]{2,1,0:T(8,128)S(1)} %get-tuple-element.20), channel_id=1, replica_groups=mesh['z'=16,'y'=4,'core'=2,'x'=4] {'y','core','x'}, dimensions={0} | all-to-all | bytes 524288 | tf_op jit(solution)/shard_map/all_to_all | solution.py:479
  63.3 20.1 %all_to_all.11.parts = f32[16,16,128]{2,1,0:T(8,128)} all-to-all(f32[16,16,128]{2,1,0:T(8,128)S(1)} %broadcast_in_dim.2), channel_id=1, replica_groups=mesh['z'=16,'y'=4,'core'=2,'x'=4] {'z'}, dimensions={0} | all-to-all | bytes 262144 | tf_op jit(solution)/shard_map/all_to_all | solution.py:481
  83.4 11.1 %solve.1 = f32[192,2048]{1,0:T(8,128)} custom-call(f32[2,6]{1,0:T(2,128)} %bitcast.9, f32[16,16,128]{2,1,0:T(8,128)} %all_to_all.11.parts, f32[64,48]{1,0:T(8,128)} %constant.17.clone.spread, bf16[8,128,2048]{2,1,0:T(8,128)(2,1)} %copy-done.1, bf16[8,128,2048]{2,1,0:T(8,128)(2,1)} %copy-done.2), custom_call_target="tpu_custom_call" | custom-call | tf_op jit(solution)/shard_map/solve/pallas_call | solution.py:485
  (5 shorter events, 0.1 us)
Async XLA Ops:
  1.7 10.9 %collective-permute-start = (f32[16,2,8,128]{3,2,1,0:T(8,128)}, f32[16,2,8,128]{3,2,1,0:T(8,128)S(1)}, u32[]{:S(2)}, u32[]{:S(2)}) collective-permute-start(f32[16,2,8,128]{3,2,1,0:T(8,128)} %get-tuple-element.14), channel_id=1, source_target_pairs={{1,0},{2,1},{3,2},{5,4},{6,5},{7,6},{9,8},{10,9},{11,10},{13,12},{... | collective-permute-start | bytes 393224 | tf_op jit(solution)/shard_map/ppermute | solution.py:419
  3.0 9.6 %collective-permute-start.1 = (f32[16,2,8,128]{3,2,1,0:T(8,128)}, f32[16,2,8,128]{3,2,1,0:T(8,128)S(1)}, u32[]{:S(2)}, u32[]{:S(2)}) collective-permute-start(f32[16,2,8,128]{3,2,1,0:T(8,128)} %get-tuple-element.15), channel_id=1, source_target_pairs={{0,1},{1,2},{2,3},{4,5},{5,6},{6,7},{8,9},{9,10},{10,11},{12,13},{... | collective-permute-start | bytes 393224 | tf_op jit(solution)/shard_map/ppermute | solution.py:418
  11.1 17.9 %copy-start = (f32[16,2,8,2048]{3,2,1,0:T(8,128)S(1)}, f32[16,2,8,2048]{3,2,1,0:T(8,128)}, u32[]{:S(2)}) copy-start(f32[16,2,8,2048]{3,2,1,0:T(8,128)} %fields.1.own) | copy-start | bytes 6291460
  12.8 28.2 %copy-start.3 = (f32[128,160]{1,0:T(8,128)S(1)}, f32[128,160]{1,0:T(8,128)}, u32[]{:S(2)}) copy-start(f32[128,160]{1,0:T(8,128)} %constant.16.clone.pick) | copy-start | bytes 245764
  12.8 28.2 %collective-permute-start.3 = (f32[4,2,8,2176]{3,2,1,0:T(8,128)S(1)}, f32[4,2,8,2176]{3,2,1,0:T(8,128)S(1)}, u32[]{:S(2)}, u32[]{:S(2)}) collective-permute-start(f32[4,2,8,2176]{3,2,1,0:T(8,128)S(1)} %get-tuple-element.25), channel_id=1, source_target_pairs={{0,508},{4,8},{8,4},{12,16},{16,12},{20,24},{24,20},{28,32},{32,28... | collective-permute-start | bytes 1671176 | tf_op jit(solution)/shard_map/ppermute | solution.py:435
  17.5 23.5 %collective-permute-start.2 = (f32[4,2,8,2176]{3,2,1,0:T(8,128)S(1)}, f32[4,2,8,2176]{3,2,1,0:T(8,128)S(1)}, u32[]{:S(2)}, u32[]{:S(2)}) collective-permute-start(f32[4,2,8,2176]{3,2,1,0:T(8,128)S(1)} %get-tuple-element.26), channel_id=1, source_target_pairs={{0,4},{4,0},{1,5},{5,1},{2,6},{6,2},{3,7},{7,3},{8,12},{12,8},{9,1... | collective-permute-start | bytes 1671176 | tf_op jit(solution)/shard_map/ppermute | solution.py:438
  39.0 2.0 %copy-start.1 = (bf16[8,128,2048]{2,1,0:T(8,128)(2,1)}, bf16[8,128,2048]{2,1,0:T(8,128)(2,1)S(1)}, u32[]{:S(2)}) copy-start(bf16[8,128,2048]{2,1,0:T(8,128)(2,1)S(1)} %get-tuple-element.21.middle_hbm) | copy-start | bytes 12582916
  48.1 2.0 %copy-start.2 = (bf16[8,128,2048]{2,1,0:T(8,128)(2,1)}, bf16[8,128,2048]{2,1,0:T(8,128)(2,1)S(1)}, u32[]{:S(2)}) copy-start(bf16[8,128,2048]{2,1,0:T(8,128)(2,1)S(1)} %get-tuple-element.22.edge_hbm) | copy-start | bytes 12582916

commit v4 on v3

--- a/solution.py
+++ b/solution.py
@@ -453,7 +453,7 @@
             pltpu.VMEM((mid_rows, ROWS, tile_cols), BF16),
             pltpu.SemaphoreType.DMA((14 + mid_rows,)),
         ],
-        compiler_params=params(28),
+        compiler_params=params(60),
         cost_estimate=pl.CostEstimate(flops=10**9, bytes_accessed=20 * 10**6, transcendentals=0),
         name="middle",
     )(fields, side)
@@ -472,7 +472,7 @@
             pltpu.VMEM((ROWS, ROWS), F32),
             pltpu.SemaphoreType.DMA((2 * HALO,)),
         ],
-        compiler_params=params(40),
+        compiler_params=params(60),
         name="edge",
     )(core.reshape(1), fields, side, near, across, first, second, third, partial, jnp.asarray(selection()))
 

time: 95.8 us -> 91.6 us (0.956)
  local copies, waits for them, and re-layouts: 5.36 us -> 2.3 us
  Pallas kernels: 33.4 us -> 32.1 us
    unnamed x8 -> x6, local copies, waits for them, and re-layouts: 3.92 us -> 1.01 us
    pallas_call x1, Pallas kernels: 9.92 us -> 7.73 us  [per_device(): pl.pallas_call(middle_kernel, out_shape=(jax.ShapeDtypeStruct((mid_rows,...]
  transfers between devices with their start and end apart: 4 -> 4, of which waited for: 0 -> 0; matrix products, arithmetic and copies ran while one was open for 2% -> 1% of each run, Pallas kernels for 14% -> 12%
where the time goes in v4:
time: 91.6 us; the launch traced here: 90.4 us
  blocking collectives  33.5 us (37%)
  Pallas kernels  32.1 us (35%)
  starting transfers between devices  22 us (24%)
  local copies, waits for them, and re-layouts  2.3 us (3%)
    all_to_all x1, blocking collectives, per_device(): lax.all_to_all(jnp.broadcast_to(total[None], (lax.axis_size('z'), 16, LAN...  20.1 us
    all_to_all x1, blocking collectives, per_device(): parts = lax.all_to_all(payload, ('y', 'core', 'x'), 0, 0, tiled=True)  13.5 us
    ppermute x1, starting transfers between devices, per_device(): lax.ppermute(jnp.where(core == 0, end, start), 'core', [(0, 1), (1, 0)])  11.6 us
    pallas_call x1, Pallas kernels, per_device(): pl.pallas_call(solve_kernel, out_shape=jax.ShapeDtypeStruct((CH * tile_ro...  11.1 us
    pallas_call x1, Pallas kernels, per_device(): pl.pallas_call(edge_kernel, out_shape=(jax.ShapeDtypeStruct((2 * HALO, 12...  7.96 us
    pallas_call x1, Pallas kernels, per_device(): pl.pallas_call(middle_kernel, out_shape=(jax.ShapeDtypeStruct((mid_rows,...  7.73 us
    ppermute x1, starting transfers between devices, per_device(): lax.ppermute(jnp.where(core == 0, start, end), gx, [(i, (i + 2 * (i % 2)...  4.57 us
    ppermute x1, starting transfers between devices, per_device(): from_left = lax.ppermute(right, 'x', [(i, i + 1) for i in range(gy - 1)])  4.57 us
  transfers between devices with their start and end apart: 4, of which 0 were waited for; matrix products, arithmetic and copies ran while one was open for 1% of the time, Pallas kernels for 12%

profile of v4, /device:TPU:1, one launch (start us, length us, event | category | flops | bytes accessed | tf_op | source)
XLA Modules:
  0.0 90.4 jit_solution(9714968533633975768)
XLA Ops:
  0.0 1.7 %edges.1 = (f32[16,2,8,128]{3,2,1,0:T(8,128)}, f32[16,2,8,128]{3,2,1,0:T(8,128)}) custom-call(f32[192,2048]{1,0:T(8,128)} %bitcast.5, f32[16,2048]{1,0:T(8,128)} %diffusion.3, f32[32,2048]{1,0:T(8,128)} %bitcast.7), custom_call_target="tpu_custom_call" | custom-call | tf_op jit(solution)/shard_map/edges/pallas_call | solution.py:409
  1.7 1.3 %collective-permute-start = (f32[16,2,8,128]{3,2,1,0:T(8,128)}, f32[16,2,8,128]{3,2,1,0:T(8,128)S(1)}, u32[]{:S(2)}, u32[]{:S(2)}) collective-permute-start(f32[16,2,8,128]{3,2,1,0:T(8,128)} %get-tuple-element.14), channel_id=1, source_target_pairs={{1,0},{2,1},{3,2},{5,4},{6,5},{7,6},{9,8},{10,9},{11,10},{13,12},{... | collective-permute-start | bytes 393224 | tf_op jit(solution)/shard_map/ppermute | solution.py:419
  3.0 4.6 %collective-permute-start.1 = (f32[16,2,8,128]{3,2,1,0:T(8,128)}, f32[16,2,8,128]{3,2,1,0:T(8,128)S(1)}, u32[]{:S(2)}, u32[]{:S(2)}) collective-permute-start(f32[16,2,8,128]{3,2,1,0:T(8,128)} %get-tuple-element.15), channel_id=1, source_target_pairs={{0,1},{1,2},{2,3},{4,5},{5,6},{6,7},{8,9},{9,10},{10,11},{12,13},{... | collective-permute-start | bytes 393224 | tf_op jit(solution)/shard_map/ppermute | solution.py:418
  7.6 3.6 %fields.1.own = f32[16,2,8,2048]{3,2,1,0:T(8,128)} custom-call(f32[192,2048]{1,0:T(8,128)} %bitcast.6, f32[16,2048]{1,0:T(8,128)} %diffusion.3, f32[32,2048]{1,0:T(8,128)} %bitcast.8), custom_call_target="tpu_custom_call" | custom-call | flops 1000000 | bytes 4000000 | tf_op jit(solution)/shard_map/fields/pallas_call | solution.py:421
  11.2 1.3 %fusion.2 = (f32[4,2,8,2048]{3,2,1,0:T(8,128)S(1)}, f32[4,2,8,2048]{3,2,1,0:T(8,128)S(1)}) fusion(f32[16,2,8,2048]{3,2,1,0:T(8,128)} %fields.1.own), kind=kLoop, calls=%fused_computation.6 | loop fusion | bytes 2097152 | tf_op jit(solution)/shard_map/slice | solution.py:432
  12.5 0.0 collective-permute-done
  12.5 0.0 collective-permute-done.1
  12.5 0.0 copy-start
  12.5 0.1 fusion
  12.6 4.6 %collective-permute-start.3 = (f32[4,2,8,2176]{3,2,1,0:T(8,128)S(1)}, f32[4,2,8,2176]{3,2,1,0:T(8,128)S(1)}, u32[]{:S(2)}, u32[]{:S(2)}) collective-permute-start(f32[4,2,8,2176]{3,2,1,0:T(8,128)S(1)} %get-tuple-element.25), channel_id=1, source_target_pairs={{0,508},{4,8},{8,4},{12,16},{16,12},{20,24},{24,20},{28,32},{32,28... | collective-permute-start | bytes 1671176 | tf_op jit(solution)/shard_map/ppermute | solution.py:435
  17.2 11.6 %collective-permute-start.2 = (f32[4,2,8,2176]{3,2,1,0:T(8,128)S(1)}, f32[4,2,8,2176]{3,2,1,0:T(8,128)S(1)}, u32[]{:S(2)}, u32[]{:S(2)}) collective-permute-start(f32[4,2,8,2176]{3,2,1,0:T(8,128)S(1)} %get-tuple-element.26), channel_id=1, source_target_pairs={{0,4},{4,0},{1,5},{5,1},{2,6},{6,2},{3,7},{7,3},{8,12},{12,8},{9,1... | collective-permute-start | bytes 1671176 | tf_op jit(solution)/shard_map/ppermute | solution.py:438
  28.8 0.0 copy-done
  28.8 7.7 %middle.1 = (bf16[8,128,2048]{2,1,0:T(8,128)(2,1)}, f32[6,2,8,2176]{3,2,1,0:T(8,128)}, f32[4,2,8,2176]{3,2,1,0:T(8,128)}, f32[4,2,8,2176]{3,2,1,0:T(8,128)}, f32[160,160]{1,0:T(8,128)}) custom-call(f32[16,2,8,2048]{3,2,1,0:T(8,128)} %fields.1.own, f32[16,2,8,128]{3,2,1,0:T(8,128)} %copy-done), custom_call_target="tpu_custom_call" | custom-call | flops 1000000000 | bytes 20000000 | tf_op jit(solution)/shard_map/middle/pallas_call | solution.py:439
  36.5 0.0 collective-permute-done.3.across
  36.5 0.0 copy-start.1
  36.5 0.0 collective-permute-done.2.near
  36.5 0.0 copy-start.2
  36.6 0.8 copy-done.1
  37.3 0.2 copy-done.2
  37.6 8.0 %edge.1 = (bf16[8,128,2048]{2,1,0:T(8,128)(2,1)}, f32[32,16,128]{2,1,0:T(8,128)}) custom-call(s32[1]{0:T(128)} %bitcast.1.core, f32[16,2,8,2048]{3,2,1,0:T(8,128)} %fields.1.own, f32[16,2,8,128]{3,2,1,0:T(8,128)} %copy-done, f32[4,2,8,2176]{3,2,1,0:T(8,128)} %copy-done.2, f32[4,2,8,2176]{3,2,1,0:T(8,128)} %copy-done.1, ...), custom_call_target="tpu_custom_call" | custom-call | tf_op jit(solution)/shard_map/edge/pallas_call | solution.py:460
  45.5 13.5 %all_to_all.10 = f32[32,16,128]{2,1,0:T(8,128)S(1)} all-to-all(f32[32,16,128]{2,1,0:T(8,128)} %get-tuple-element.20), channel_id=1, replica_groups=mesh['z'=16,'y'=4,'core'=2,'x'=4] {'y','core','x'}, dimensions={0} | all-to-all | bytes 524288 | tf_op jit(solution)/shard_map/all_to_all | solution.py:479
  59.0 20.1 %all_to_all.11.parts = f32[16,16,128]{2,1,0:T(8,128)} all-to-all(f32[16,16,128]{2,1,0:T(8,128)S(1)} %broadcast_in_dim.2), channel_id=1, replica_groups=mesh['z'=16,'y'=4,'core'=2,'x'=4] {'z'}, dimensions={0} | all-to-all | bytes 262144 | tf_op jit(solution)/shard_map/all_to_all | solution.py:481
  79.1 11.1 %solve.1 = f32[192,2048]{1,0:T(8,128)} custom-call(f32[2,6]{1,0:T(2,128)} %bitcast.9, f32[16,16,128]{2,1,0:T(8,128)} %all_to_all.11.parts, f32[64,48]{1,0:T(8,128)} %constant.17.clone.spread, bf16[8,128,2048]{2,1,0:T(8,128)(2,1)} %get-tuple-element.21.middle_hbm, bf16[8,128,2048]{2,1,0:T(8,128)(2,1)} %get-tuple-element.22.edge_hbm), custom_call_target="tpu_custom_call" | custom-call | tf_op jit(solution)/shard_map/solve/pallas_call | solution.py:485
  (5 shorter events, 0.1 us)
Async XLA Ops:
  1.7 10.7 %collective-permute-start = (f32[16,2,8,128]{3,2,1,0:T(8,128)}, f32[16,2,8,128]{3,2,1,0:T(8,128)S(1)}, u32[]{:S(2)}, u32[]{:S(2)}) collective-permute-start(f32[16,2,8,128]{3,2,1,0:T(8,128)} %get-tuple-element.14), channel_id=1, source_target_pairs={{1,0},{2,1},{3,2},{5,4},{6,5},{7,6},{9,8},{10,9},{11,10},{13,12},{... | collective-permute-start | bytes 393224 | tf_op jit(solution)/shard_map/ppermute | solution.py:419
  3.0 9.5 %collective-permute-start.1 = (f32[16,2,8,128]{3,2,1,0:T(8,128)}, f32[16,2,8,128]{3,2,1,0:T(8,128)S(1)}, u32[]{:S(2)}, u32[]{:S(2)}) collective-permute-start(f32[16,2,8,128]{3,2,1,0:T(8,128)} %get-tuple-element.15), channel_id=1, source_target_pairs={{0,1},{1,2},{2,3},{4,5},{5,6},{6,7},{8,9},{9,10},{10,11},{12,13},{... | collective-permute-start | bytes 393224 | tf_op jit(solution)/shard_map/ppermute | solution.py:418
  12.5 16.3 %copy-start = (f32[16,2,8,128]{3,2,1,0:T(8,128)}, f32[16,2,8,128]{3,2,1,0:T(8,128)S(1)}, u32[]{:S(2)}) copy-start(f32[16,2,8,128]{3,2,1,0:T(8,128)S(1)} %broadcast_select_fusion.side) | copy-start | bytes 393220
  12.6 23.9 %collective-permute-start.3 = (f32[4,2,8,2176]{3,2,1,0:T(8,128)S(1)}, f32[4,2,8,2176]{3,2,1,0:T(8,128)S(1)}, u32[]{:S(2)}, u32[]{:S(2)}) collective-permute-start(f32[4,2,8,2176]{3,2,1,0:T(8,128)S(1)} %get-tuple-element.25), channel_id=1, source_target_pairs={{0,508},{4,8},{8,4},{12,16},{16,12},{20,24},{24,20},{28,32},{32,28... | collective-permute-start | bytes 1671176 | tf_op jit(solution)/shard_map/ppermute | solution.py:435
  17.2 19.3 %collective-permute-start.2 = (f32[4,2,8,2176]{3,2,1,0:T(8,128)S(1)}, f32[4,2,8,2176]{3,2,1,0:T(8,128)S(1)}, u32[]{:S(2)}, u32[]{:S(2)}) collective-permute-start(f32[4,2,8,2176]{3,2,1,0:T(8,128)S(1)} %get-tuple-element.26), channel_id=1, source_target_pairs={{0,4},{4,0},{1,5},{5,1},{2,6},{6,2},{3,7},{7,3},{8,12},{12,8},{9,1... | collective-permute-start | bytes 1671176 | tf_op jit(solution)/shard_map/ppermute | solution.py:438
  36.5 0.8 copy-start.1
  36.5 1.0 %copy-start.2 = (f32[4,2,8,2176]{3,2,1,0:T(8,128)}, f32[4,2,8,2176]{3,2,1,0:T(8,128)S(1)}, u32[]{:S(2)}) copy-start(f32[4,2,8,2176]{3,2,1,0:T(8,128)S(1)} %collective-permute-done.2.near) | copy-start | bytes 1671172

commit v5 on v4

--- a/solution.py
+++ b/solution.py
@@ -301,43 +301,43 @@
         rhs_imag = alpha_i * g2 + b * g1 + SCALE * gd2
         real = jnp.where(inside, real, jnp.where(at_rhs, rhs_real, 0.0))
         imag = jnp.where(inside, imag, jnp.where(at_rhs, rhs_imag, 0.0))
-        system = real + pltpu.roll(imag, 64, 1)
-        systems.append([system[8 * i : 8 * i + 8] for i in range(6)])
-    return systems
-
-
-def column_of(block, at):
-    return jnp.broadcast_to(block[:, at : at + 1], (8, 128))
-
-
-def eliminate(systems):
-    flip = jnp.where(lane((1, 128)) < 64, -1.0, 1.0)
+        systems.append((real, imag))
+    left = lanes < 64
+    pairs = []
+    for first, second in zip(systems[::2], systems[1::2]):
+        both = [jnp.where(left, f, pltpu.roll(g, 64, 1)) for f, g in zip(first, second)]
+        pairs.append([[part[8 * i : 8 * i + 8] for i in range(6)] for part in both])
+    return pairs
+
+
+def eliminate(pairs):
+    lanes = lane((8, 128))
     rows_id = lax.broadcasted_iota(jnp.int32, (8, 128), 0)
     for k in range(0, 48, 2):
         at, p = k // 8, k % 8
-        for blocks in systems:
-            pivot = blocks[at]
-            row0, row1 = pivot[p : p + 1], pivot[p + 1 : p + 2]
-            turn0 = pltpu.roll(row0, 64, 1) * flip
-            turn1 = pltpu.roll(row1, 64, 1) * flip
+        where = jnp.where(lanes < 64, k, 64 + k)
+        for pair in pairs:
             columns = [
-                [column_of(b, c) for c in (k, 64 + k, k + 1, 65 + k)] for b in blocks
+                [jnp.take_along_axis(part[i], where + n, axis=1) for part in pair] for n in range(2) for i in range(6)
             ]
-            c0r, _, c1r, c1i = columns[at]
-            a, zr, zi, d = c0r[p : p + 1], c1r[p : p + 1], c1i[p : p + 1], c1r[p + 1 : p + 2]
+            (a, _), (zr, zi), (d, _) = columns[at], columns[6 + at], columns[6 + at]
+            a, zr, zi, d = a[p : p + 1], zr[p : p + 1], zi[p : p + 1], d[p + 1 : p + 2]
             scale = 1.0 / (a * d - (zr * zr + zi * zi))
             a, zr, zi, d = a * scale, zr * scale, zi * scale, d * scale
-            x0 = d * row0 - (zr * row1 + zi * turn1)
-            x1 = a * row1 - (zr * row0 - zi * turn0)
-            t0 = d * turn0 - (zr * turn1 - zi * row1)
-            t1 = a * turn1 - (zr * turn0 + zi * row0)
+            r0, i0, r1, i1 = (pair[part][at][p + n : p + n + 1] for n in range(2) for part in range(2))
+            xr0 = d * r0 - (zr * r1 - zi * i1)
+            xi0 = d * i0 - (zr * i1 + zi * r1)
+            xr1 = a * r1 - (zr * r0 + zi * i0)
+            xi1 = a * i1 - (zr * i0 - zi * r0)
             for i in range(6):
-                c0r, c0i, c1r, c1i = columns[i]
-                update = blocks[i] - ((c0r * x0 + c0i * t0) + (c1r * x1 + c1i * t1))
+                (cr0, ci0), (cr1, ci1) = columns[i], columns[6 + i]
+                real = pair[0][i] - ((cr0 * xr0 - ci0 * xi0) + (cr1 * xr1 - ci1 * xi1))
+                imag = pair[1][i] - ((cr0 * xi0 + ci0 * xr0) + (cr1 * xi1 + ci1 * xr1))
                 if i == at:
-                    update = jnp.where(rows_id == p, x0, jnp.where(rows_id == p + 1, x1, update))
-                blocks[i] = update
-    return systems
+                    real = jnp.where(rows_id == p, xr0, jnp.where(rows_id == p + 1, xr1, real))
+                    imag = jnp.where(rows_id == p, xi0, jnp.where(rows_id == p + 1, xi1, imag))
+                pair[0][i], pair[1][i] = real, imag
+    return pairs
 
 
 def solve_kernel(shifts, parts, spread, middle_hbm, edge_hbm, out, middle, edge, mixed, sems):
@@ -350,13 +350,15 @@
     for copy in copies:
         copy.start()
 
-    systems = eliminate(normal_systems(unpack(parts), shifts))
+    pairs = eliminate(normal_systems(unpack(parts), shifts))
     lanes = lane((48, 128))
     mix = jnp.zeros((48, 128), F32)
-    for j, blocks in enumerate(systems):
-        m = jnp.concatenate(blocks, axis=0)
-        mix = jnp.where(lanes == 2 * j, jnp.broadcast_to(m[:, 48:49], (48, 128)), mix)
-        mix = jnp.where(lanes == 2 * j + 1, jnp.broadcast_to(m[:, 112:113], (48, 128)), mix)
+    for q, pair in enumerate(pairs):
+        for n, part in enumerate(pair):
+            m = jnp.concatenate(part, axis=0)
+            for side in range(2):
+                at = 48 + 64 * side
+                mix = jnp.where(lanes == 4 * q + 2 * side + n, jnp.broadcast_to(m[:, at : at + 1], (48, 128)), mix)
     mix = jnp.dot(spread[...], mix, precision=HIGH, preferred_element_type=F32)
     mix_hi, mix_lo = split(mix)
     weights = mix_hi.astype(F32) + pltpu.roll(mix_lo.astype(F32), 16, 1)

time: 91.6 us -> 89.2 us (0.974)
  Pallas kernels: 32.1 us -> 29.7 us
    pallas_call x1, Pallas kernels: 11.1 us -> 8.72 us  [per_device(): pl.pallas_call(solve_kernel, out_shape=jax.ShapeDtypeStruct((CH * tile_ro...]
  transfers between devices with their start and end apart: 4 -> 4, of which waited for: 0 -> 0; matrix products, arithmetic and copies ran while one was open for 1% -> 1% of each run, Pallas kernels for 12% -> 13%
where the time goes in v5:
time: 89.2 us; the launch traced here: 88 us
  blocking collectives  33.5 us (38%)
  Pallas kernels  29.7 us (33%)
  starting transfers between devices  22 us (25%)
  local copies, waits for them, and re-layouts  2.3 us (3%)
    all_to_all x1, blocking collectives, per_device(): lax.all_to_all(jnp.broadcast_to(total[None], (lax.axis_size('z'), 16, LAN...  20.1 us
    all_to_all x1, blocking collectives, per_device(): parts = lax.all_to_all(payload, ('y', 'core', 'x'), 0, 0, tiled=True)  13.5 us
    ppermute x1, starting transfers between devices, per_device(): lax.ppermute(jnp.where(core == 0, end, start), 'core', [(0, 1), (1, 0)])  11.6 us
    pallas_call x1, Pallas kernels, per_device(): pl.pallas_call(solve_kernel, out_shape=jax.ShapeDtypeStruct((CH * tile_ro...  8.72 us
    pallas_call x1, Pallas kernels, per_device(): pl.pallas_call(edge_kernel, out_shape=(jax.ShapeDtypeStruct((2 * HALO, 12...  7.96 us
    pallas_call x1, Pallas kernels, per_device(): pl.pallas_call(middle_kernel, out_shape=(jax.ShapeDtypeStruct((mid_rows,...  7.73 us
    ppermute x1, starting transfers between devices, per_device(): from_left = lax.ppermute(right, 'x', [(i, i + 1) for i in range(gy - 1)])  4.57 us
    ppermute x1, starting transfers between devices, per_device(): lax.ppermute(jnp.where(core == 0, start, end), gx, [(i, (i + 2 * (i % 2)...  4.57 us
  transfers between devices with their start and end apart: 4, of which 0 were waited for; matrix products, arithmetic and copies ran while one was open for 1% of the time, Pallas kernels for 13%

profile of v5, /device:TPU:1, one launch (start us, length us, event | category | flops | bytes accessed | tf_op | source)
XLA Modules:
  0.0 88.0 jit_solution(1203742076577128666)
XLA Ops:
  0.0 1.7 %edges.1 = (f32[16,2,8,128]{3,2,1,0:T(8,128)}, f32[16,2,8,128]{3,2,1,0:T(8,128)}) custom-call(f32[192,2048]{1,0:T(8,128)} %bitcast.5, f32[16,2048]{1,0:T(8,128)} %diffusion.3, f32[32,2048]{1,0:T(8,128)} %bitcast.7), custom_call_target="tpu_custom_call" | custom-call | tf_op jit(solution)/shard_map/edges/pallas_call | solution.py:411
  1.7 1.3 %collective-permute-start = (f32[16,2,8,128]{3,2,1,0:T(8,128)}, f32[16,2,8,128]{3,2,1,0:T(8,128)S(1)}, u32[]{:S(2)}, u32[]{:S(2)}) collective-permute-start(f32[16,2,8,128]{3,2,1,0:T(8,128)} %get-tuple-element.14), channel_id=1, source_target_pairs={{1,0},{2,1},{3,2},{5,4},{6,5},{7,6},{9,8},{10,9},{11,10},{13,12},{... | collective-permute-start | bytes 393224 | tf_op jit(solution)/shard_map/ppermute | solution.py:421
  3.0 4.6 %collective-permute-start.1 = (f32[16,2,8,128]{3,2,1,0:T(8,128)}, f32[16,2,8,128]{3,2,1,0:T(8,128)S(1)}, u32[]{:S(2)}, u32[]{:S(2)}) collective-permute-start(f32[16,2,8,128]{3,2,1,0:T(8,128)} %get-tuple-element.15), channel_id=1, source_target_pairs={{0,1},{1,2},{2,3},{4,5},{5,6},{6,7},{8,9},{9,10},{10,11},{12,13},{... | collective-permute-start | bytes 393224 | tf_op jit(solution)/shard_map/ppermute | solution.py:420
  7.6 3.6 %fields.1.own = f32[16,2,8,2048]{3,2,1,0:T(8,128)} custom-call(f32[192,2048]{1,0:T(8,128)} %bitcast.6, f32[16,2048]{1,0:T(8,128)} %diffusion.3, f32[32,2048]{1,0:T(8,128)} %bitcast.8), custom_call_target="tpu_custom_call" | custom-call | flops 1000000 | bytes 4000000 | tf_op jit(solution)/shard_map/fields/pallas_call | solution.py:423
  11.2 1.3 %fusion.2 = (f32[4,2,8,2048]{3,2,1,0:T(8,128)S(1)}, f32[4,2,8,2048]{3,2,1,0:T(8,128)S(1)}) fusion(f32[16,2,8,2048]{3,2,1,0:T(8,128)} %fields.1.own), kind=kLoop, calls=%fused_computation.6 | loop fusion | bytes 2097152 | tf_op jit(solution)/shard_map/slice | solution.py:434
  12.5 0.0 collective-permute-done
  12.5 0.0 collective-permute-done.1
  12.5 0.0 copy-start
  12.5 0.1 fusion
  12.6 4.6 %collective-permute-start.3 = (f32[4,2,8,2176]{3,2,1,0:T(8,128)S(1)}, f32[4,2,8,2176]{3,2,1,0:T(8,128)S(1)}, u32[]{:S(2)}, u32[]{:S(2)}) collective-permute-start(f32[4,2,8,2176]{3,2,1,0:T(8,128)S(1)} %get-tuple-element.25), channel_id=1, source_target_pairs={{0,508},{4,8},{8,4},{12,16},{16,12},{20,24},{24,20},{28,32},{32,28... | collective-permute-start | bytes 1671176 | tf_op jit(solution)/shard_map/ppermute | solution.py:437
  17.2 11.6 %collective-permute-start.2 = (f32[4,2,8,2176]{3,2,1,0:T(8,128)S(1)}, f32[4,2,8,2176]{3,2,1,0:T(8,128)S(1)}, u32[]{:S(2)}, u32[]{:S(2)}) collective-permute-start(f32[4,2,8,2176]{3,2,1,0:T(8,128)S(1)} %get-tuple-element.26), channel_id=1, source_target_pairs={{0,4},{4,0},{1,5},{5,1},{2,6},{6,2},{3,7},{7,3},{8,12},{12,8},{9,1... | collective-permute-start | bytes 1671176 | tf_op jit(solution)/shard_map/ppermute | solution.py:440
  28.8 0.0 copy-done
  28.8 7.7 %middle.1 = (bf16[8,128,2048]{2,1,0:T(8,128)(2,1)}, f32[6,2,8,2176]{3,2,1,0:T(8,128)}, f32[4,2,8,2176]{3,2,1,0:T(8,128)}, f32[4,2,8,2176]{3,2,1,0:T(8,128)}, f32[160,160]{1,0:T(8,128)}) custom-call(f32[16,2,8,2048]{3,2,1,0:T(8,128)} %fields.1.own, f32[16,2,8,128]{3,2,1,0:T(8,128)} %copy-done), custom_call_target="tpu_custom_call" | custom-call | flops 1000000000 | bytes 20000000 | tf_op jit(solution)/shard_map/middle/pallas_call | solution.py:441
  36.5 0.0 collective-permute-done.3.across
  36.5 0.0 copy-start.1
  36.5 0.0 collective-permute-done.2.near
  36.5 0.0 copy-start.2
  36.6 0.8 copy-done.1
  37.3 0.2 copy-done.2
  37.6 8.0 %edge.1 = (bf16[8,128,2048]{2,1,0:T(8,128)(2,1)}, f32[32,16,128]{2,1,0:T(8,128)}) custom-call(s32[1]{0:T(128)} %bitcast.1.core, f32[16,2,8,2048]{3,2,1,0:T(8,128)} %fields.1.own, f32[16,2,8,128]{3,2,1,0:T(8,128)} %copy-done, f32[4,2,8,2176]{3,2,1,0:T(8,128)} %copy-done.2, f32[4,2,8,2176]{3,2,1,0:T(8,128)} %copy-done.1, ...), custom_call_target="tpu_custom_call" | custom-call | tf_op jit(solution)/shard_map/edge/pallas_call | solution.py:462
  45.5 13.5 %all_to_all.10 = f32[32,16,128]{2,1,0:T(8,128)S(1)} all-to-all(f32[32,16,128]{2,1,0:T(8,128)} %get-tuple-element.20), channel_id=1, replica_groups=mesh['z'=16,'y'=4,'core'=2,'x'=4] {'y','core','x'}, dimensions={0} | all-to-all | bytes 524288 | tf_op jit(solution)/shard_map/all_to_all | solution.py:481
  59.0 20.1 %all_to_all.11.parts = f32[16,16,128]{2,1,0:T(8,128)} all-to-all(f32[16,16,128]{2,1,0:T(8,128)S(1)} %broadcast_in_dim.2), channel_id=1, replica_groups=mesh['z'=16,'y'=4,'core'=2,'x'=4] {'z'}, dimensions={0} | all-to-all | bytes 262144 | tf_op jit(solution)/shard_map/all_to_all | solution.py:483
  79.1 8.7 %solve.1 = f32[192,2048]{1,0:T(8,128)} custom-call(f32[2,6]{1,0:T(2,128)} %bitcast.9, f32[16,16,128]{2,1,0:T(8,128)} %all_to_all.11.parts, f32[64,48]{1,0:T(8,128)} %constant.17.clone.spread, bf16[8,128,2048]{2,1,0:T(8,128)(2,1)} %get-tuple-element.21.middle_hbm, bf16[8,128,2048]{2,1,0:T(8,128)(2,1)} %get-tuple-element.22.edge_hbm), custom_call_target="tpu_custom_call" | custom-call | tf_op jit(solution)/shard_map/solve/pallas_call | solution.py:487
  (5 shorter events, 0.1 us)
Async XLA Ops:
  1.7 10.7 %collective-permute-start = (f32[16,2,8,128]{3,2,1,0:T(8,128)}, f32[16,2,8,128]{3,2,1,0:T(8,128)S(1)}, u32[]{:S(2)}, u32[]{:S(2)}) collective-permute-start(f32[16,2,8,128]{3,2,1,0:T(8,128)} %get-tuple-element.14), channel_id=1, source_target_pairs={{1,0},{2,1},{3,2},{5,4},{6,5},{7,6},{9,8},{10,9},{11,10},{13,12},{... | collective-permute-start | bytes 393224 | tf_op jit(solution)/shard_map/ppermute | solution.py:421
  3.0 9.5 %collective-permute-start.1 = (f32[16,2,8,128]{3,2,1,0:T(8,128)}, f32[16,2,8,128]{3,2,1,0:T(8,128)S(1)}, u32[]{:S(2)}, u32[]{:S(2)}) collective-permute-start(f32[16,2,8,128]{3,2,1,0:T(8,128)} %get-tuple-element.15), channel_id=1, source_target_pairs={{0,1},{1,2},{2,3},{4,5},{5,6},{6,7},{8,9},{9,10},{10,11},{12,13},{... | collective-permute-start | bytes 393224 | tf_op jit(solution)/shard_map/ppermute | solution.py:420
  12.5 16.3 %copy-start = (f32[16,2,8,128]{3,2,1,0:T(8,128)}, f32[16,2,8,128]{3,2,1,0:T(8,128)S(1)}, u32[]{:S(2)}) copy-start(f32[16,2,8,128]{3,2,1,0:T(8,128)S(1)} %broadcast_select_fusion.side) | copy-start | bytes 393220
  12.6 23.9 %collective-permute-start.3 = (f32[4,2,8,2176]{3,2,1,0:T(8,128)S(1)}, f32[4,2,8,2176]{3,2,1,0:T(8,128)S(1)}, u32[]{:S(2)}, u32[]{:S(2)}) collective-permute-start(f32[4,2,8,2176]{3,2,1,0:T(8,128)S(1)} %get-tuple-element.25), channel_id=1, source_target_pairs={{0,508},{4,8},{8,4},{12,16},{16,12},{20,24},{24,20},{28,32},{32,28... | collective-permute-start | bytes 1671176 | tf_op jit(solution)/shard_map/ppermute | solution.py:437
  17.2 19.3 %collective-permute-start.2 = (f32[4,2,8,2176]{3,2,1,0:T(8,128)S(1)}, f32[4,2,8,2176]{3,2,1,0:T(8,128)S(1)}, u32[]{:S(2)}, u32[]{:S(2)}) collective-permute-start(f32[4,2,8,2176]{3,2,1,0:T(8,128)S(1)} %get-tuple-element.26), channel_id=1, source_target_pairs={{0,4},{4,0},{1,5},{5,1},{2,6},{6,2},{3,7},{7,3},{8,12},{12,8},{9,1... | collective-permute-start | bytes 1671176 | tf_op jit(solution)/shard_map/ppermute | solution.py:440
  36.5 0.8 copy-start.1
  36.5 1.0 %copy-start.2 = (f32[4,2,8,2176]{3,2,1,0:T(8,128)}, f32[4,2,8,2176]{3,2,1,0:T(8,128)S(1)}, u32[]{:S(2)}) copy-start(f32[4,2,8,2176]{3,2,1,0:T(8,128)S(1)} %collective-permute-done.2.near) | copy-start | bytes 1671172

commit v6 on v5

--- a/solution.py
+++ b/solution.py
@@ -215,33 +215,40 @@
     return copies
 
 
-def edges_kernel(right_side, diffusion, drift_field, left, right, strips, sems):
+def edges_kernel(place, right_side, diffusion, drift_field, inner, outer, strips, sems):
     tile_rows, tile_cols = diffusion.shape
-    outs = (left, right)
+    even = lax.rem(place[0], 2) == 0
     places = (0, tile_cols // LANE - 1)
     copies = [gather_rows(right_side, diffusion, drift_field, strips, sems, (i, p)) for i, p in enumerate(places)]
     for i in range(2):
         strips[i, 15 * tile_rows :] = jnp.zeros((tile_rows, LANE), F32)
         for copy in copies[i]:
             copy.wait()
-        for r in range(tile_rows):
-            for half in range(2):
-                outs[i][r, half] = strips.at[i][pl.ds(8 * half * tile_rows + r, 8, stride=tile_rows), :]
-
-
-def fields_kernel(right_side, diffusion, drift_field, fields, strips, sems):
+    for r in range(tile_rows):
+        for half in range(2):
+            rows = pl.ds(8 * half * tile_rows + r, 8, stride=tile_rows)
+            first, last = strips.at[0][rows, :], strips.at[1][rows, :]
+            inner[r, half] = jnp.where(even, last, first)
+            outer[r, half] = jnp.where(even, first, last)
+
+
+def fields_kernel(right_side, diffusion, drift_field, fields, strips, turned, sems, out_sems):
     tile_rows, tile_cols = diffusion.shape
     count = tile_cols // LANE
     copies = [gather_rows(right_side, diffusion, drift_field, strips, sems, (i, i)) for i in range(count)]
+    finished = []
     for i in range(count):
         strips[i, 15 * tile_rows :] = jnp.zeros((tile_rows, LANE), F32)
         for copy in copies[i]:
             copy.wait()
         for r in range(tile_rows):
             for half in range(2):
-                fields[r, half, :, i * LANE : (i + 1) * LANE] = strips.at[i][
-                    pl.ds(8 * half * tile_rows + r, 8, stride=tile_rows), :
-                ]
+                turned[i, r, half] = strips.at[i][pl.ds(8 * half * tile_rows + r, 8, stride=tile_rows), :]
+        copy = pltpu.make_async_copy(turned.at[i], fields.at[:, :, :, pl.ds(i * LANE, LANE)], out_sems.at[i])
+        copy.start()
+        finished.append(copy)
+    for copy in finished:
+        copy.wait()
 
 
 def lane(shape):
@@ -408,23 +415,31 @@
         diffusion,
         drift_field.reshape(2 * tile_rows, tile_cols),
     )
-    left, right = pl.pallas_call(
+    place = lax.axis_index("x")
+    inner, outer = pl.pallas_call(
         edges_kernel,
         out_shape=[jax.ShapeDtypeStruct(rows_of(tile_rows, LANE), F32)] * 2,
-        in_specs=[anywhere] * 3,
+        in_specs=[scalar, *[anywhere] * 3],
         scratch_shapes=[pltpu.VMEM((2, 16 * tile_rows, LANE), F32), pltpu.SemaphoreType.DMA((2, 3))],
         compiler_params=params(60),
         name="edges",
-    )(*raw)
+    )(place.reshape(1), *raw)
     gy = lax.axis_size("x")
-    from_left = lax.ppermute(right, "x", [(i, i + 1) for i in range(gy - 1)])
-    from_right = lax.ppermute(left, "x", [(i + 1, i) for i in range(gy - 1)])
-    side = jnp.where(lax.broadcasted_iota(jnp.int32, from_left.shape, 3) < LANE // 2, from_right, from_left)
+    inner = lax.ppermute(inner, "x", [(i, i ^ 1) for i in range(gy)])
+    outer = lax.ppermute(outer, "x", [(i, i + 2 * (i % 2) - 1) for i in range(1, gy - 1)])
+    after = lax.broadcasted_iota(jnp.int32, inner.shape, 3) < LANE // 2
+    side = jnp.where(after == (place % 2 == 0), inner, outer)
     fields = pl.pallas_call(
         fields_kernel,
         out_shape=jax.ShapeDtypeStruct(rows_of(tile_rows, tile_cols), F32),
         in_specs=[anywhere] * 3,
-        scratch_shapes=[pltpu.VMEM((count, 16 * tile_rows, LANE), F32), pltpu.SemaphoreType.DMA((count, 3))],
+        out_specs=far,
+        scratch_shapes=[
+            pltpu.VMEM((count, 16 * tile_rows, LANE), F32),
+            pltpu.VMEM((count, *rows_of(tile_rows, LANE)), F32),
+            pltpu.SemaphoreType.DMA((count, 3)),
+            pltpu.SemaphoreType.DMA((count,)),
+        ],
         compiler_params=params(60),
         cost_estimate=pl.CostEstimate(flops=10**6, bytes_accessed=4 * 10**6, transcendentals=0),
         name="fields",

time: 89.2 us -> 88.7 us (level)
  starting transfers between devices: 22 us -> 20.5 us
  blocking collectives: 33.5 us -> 34.9 us
    ppermute x2, starting transfers between devices: 5.86 us -> 4.61 us  [the longest x1 3.94 us: per_device(): inner = lax.ppermute(inner, 'x', [(i, i ^ 1) for i in range(gy)])]
    all_to_all x1, blocking collectives: 13.5 us -> 14.4 us  [per_device(): parts = lax.all_to_all(payload, ('y', 'core', 'x'), 0, 0, tiled=True)]
  transfers between devices with their start and end apart: 4 -> 4, of which waited for: 0 -> 0; matrix products, arithmetic and copies ran while one was open for 1% -> 1% of each run, Pallas kernels for 13% -> 12%
where the time goes in v6:
time: 88.7 us; the launch traced here: 87.5 us
  blocking collectives  34.9 us (39%)
  Pallas kernels  29.3 us (33%)
  starting transfers between devices  20.5 us (23%)
  local copies, waits for them, and re-layouts  2.3 us (3%)
    all_to_all x1, blocking collectives, per_device(): lax.all_to_all(jnp.broadcast_to(total[None], (lax.axis_size('z'), 16, LAN...  20.5 us
    all_to_all x1, blocking collectives, per_device(): parts = lax.all_to_all(payload, ('y', 'core', 'x'), 0, 0, tiled=True)  14.4 us
    ppermute x1, starting transfers between devices, per_device(): lax.ppermute(jnp.where(core == 0, end, start), 'core', [(0, 1), (1, 0)])  11.8 us
    pallas_call x1, Pallas kernels, per_device(): pl.pallas_call(solve_kernel, out_shape=jax.ShapeDtypeStruct((CH * tile_ro...  8.71 us
    pallas_call x1, Pallas kernels, per_device(): pl.pallas_call(edge_kernel, out_shape=(jax.ShapeDtypeStruct((2 * HALO, 12...  7.96 us
    pallas_call x1, Pallas kernels, per_device(): pl.pallas_call(middle_kernel, out_shape=(jax.ShapeDtypeStruct((mid_rows,...  7.73 us
    ppermute x1, starting transfers between devices, per_device(): lax.ppermute(jnp.where(core == 0, start, end), gx, [(i, (i + 2 * (i % 2)...  4.05 us
    ppermute x1, starting transfers between devices, per_device(): inner = lax.ppermute(inner, 'x', [(i, i ^ 1) for i in range(gy)])  3.94 us
  transfers between devices with their start and end apart: 4, of which 0 were waited for; matrix products, arithmetic and copies ran while one was open for 1% of the time, Pallas kernels for 12%

profile of v6, /device:TPU:1, one launch (start us, length us, event | category | flops | bytes accessed | tf_op | source)
XLA Modules:
  0.0 87.5 jit_solution(7741781624986274414)
XLA Ops:
  0.0 1.8 %edges.1 = (f32[16,2,8,128]{3,2,1,0:T(8,128)}, f32[16,2,8,128]{3,2,1,0:T(8,128)}) custom-call(s32[1]{0:T(128)} %bitcast.4.place, f32[192,2048]{1,0:T(8,128)} %bitcast.6, f32[16,2048]{1,0:T(8,128)} %diffusion.3, f32[32,2048]{1,0:T(8,128)} %bitcast.8), custom_call_target="tpu_custom_call" | custom-call | tf_op jit(solution)/shard_map/edges/pallas_call | solution.py:419
  1.8 3.9 %collective-permute-start = (f32[16,2,8,128]{3,2,1,0:T(8,128)}, f32[16,2,8,128]{3,2,1,0:T(8,128)S(1)}, u32[]{:S(2)}, u32[]{:S(2)}) collective-permute-start(f32[16,2,8,128]{3,2,1,0:T(8,128)} %get-tuple-element.14), channel_id=1, source_target_pairs={{0,1},{1,0},{2,3},{3,2},{4,5},{5,4},{6,7},{7,6},{8,9},{9,8},{10,11... | collective-permute-start | bytes 393224 | tf_op jit(solution)/shard_map/ppermute | solution.py:428
  5.7 0.7 collective-permute-start.1
  6.4 3.1 %fields.1.own = f32[16,2,8,2048]{3,2,1,0:T(8,128)} custom-call(f32[192,2048]{1,0:T(8,128)} %bitcast.7, f32[16,2048]{1,0:T(8,128)} %diffusion.3, f32[32,2048]{1,0:T(8,128)} %bitcast.9), custom_call_target="tpu_custom_call" | custom-call | flops 1000000 | bytes 4000000 | tf_op jit(solution)/shard_map/fields/pallas_call | solution.py:432
  9.5 1.3 %fusion.2 = (f32[4,2,8,2048]{3,2,1,0:T(8,128)S(1)}, f32[4,2,8,2048]{3,2,1,0:T(8,128)S(1)}) fusion(f32[16,2,8,2048]{3,2,1,0:T(8,128)} %fields.1.own), kind=kLoop, calls=%fused_computation.6 | loop fusion | bytes 2097152 | tf_op jit(solution)/shard_map/slice | solution.py:449
  10.8 0.0 collective-permute-done
  10.8 0.0 collective-permute-done.1
  10.9 0.0 copy-start
  10.9 0.1 fusion
  11.0 4.0 %collective-permute-start.3 = (f32[4,2,8,2176]{3,2,1,0:T(8,128)S(1)}, f32[4,2,8,2176]{3,2,1,0:T(8,128)S(1)}, u32[]{:S(2)}, u32[]{:S(2)}) collective-permute-start(f32[4,2,8,2176]{3,2,1,0:T(8,128)S(1)} %get-tuple-element.25), channel_id=1, source_target_pairs={{0,508},{4,8},{8,4},{12,16},{16,12},{20,24},{24,20},{28,32},{32,28... | collective-permute-start | bytes 1671176 | tf_op jit(solution)/shard_map/ppermute | solution.py:452
  15.0 11.8 %collective-permute-start.2 = (f32[4,2,8,2176]{3,2,1,0:T(8,128)S(1)}, f32[4,2,8,2176]{3,2,1,0:T(8,128)S(1)}, u32[]{:S(2)}, u32[]{:S(2)}) collective-permute-start(f32[4,2,8,2176]{3,2,1,0:T(8,128)S(1)} %get-tuple-element.26), channel_id=1, source_target_pairs={{0,4},{4,0},{1,5},{5,1},{2,6},{6,2},{3,7},{7,3},{8,12},{12,8},{9,1... | collective-permute-start | bytes 1671176 | tf_op jit(solution)/shard_map/ppermute | solution.py:455
  26.9 0.0 copy-done
  26.9 7.7 %middle.1 = (bf16[8,128,2048]{2,1,0:T(8,128)(2,1)}, f32[6,2,8,2176]{3,2,1,0:T(8,128)}, f32[4,2,8,2176]{3,2,1,0:T(8,128)}, f32[4,2,8,2176]{3,2,1,0:T(8,128)}, f32[160,160]{1,0:T(8,128)}) custom-call(f32[16,2,8,2048]{3,2,1,0:T(8,128)} %fields.1.own, f32[16,2,8,128]{3,2,1,0:T(8,128)} %copy-done), custom_call_target="tpu_custom_call" | custom-call | flops 1000000000 | bytes 20000000 | tf_op jit(solution)/shard_map/middle/pallas_call | solution.py:456
  34.6 0.0 collective-permute-done.3.across
  34.6 0.0 copy-start.1
  34.7 0.0 collective-permute-done.2.near
  34.7 0.0 copy-start.2
  34.7 0.8 copy-done.1
  35.5 0.2 copy-done.2
  35.7 8.0 %edge.1 = (bf16[8,128,2048]{2,1,0:T(8,128)(2,1)}, f32[32,16,128]{2,1,0:T(8,128)}) custom-call(s32[1]{0:T(128)} %bitcast.1.core, f32[16,2,8,2048]{3,2,1,0:T(8,128)} %fields.1.own, f32[16,2,8,128]{3,2,1,0:T(8,128)} %copy-done, f32[4,2,8,2176]{3,2,1,0:T(8,128)} %copy-done.2, f32[4,2,8,2176]{3,2,1,0:T(8,128)} %copy-done.1, ...), custom_call_target="tpu_custom_call" | custom-call | tf_op jit(solution)/shard_map/edge/pallas_call | solution.py:477
  43.6 14.4 %all_to_all.10 = f32[32,16,128]{2,1,0:T(8,128)S(1)} all-to-all(f32[32,16,128]{2,1,0:T(8,128)} %get-tuple-element.20), channel_id=1, replica_groups=mesh['z'=16,'y'=4,'core'=2,'x'=4] {'y','core','x'}, dimensions={0} | all-to-all | bytes 524288 | tf_op jit(solution)/shard_map/all_to_all | solution.py:496
  58.1 20.5 %all_to_all.11.parts = f32[16,16,128]{2,1,0:T(8,128)} all-to-all(f32[16,16,128]{2,1,0:T(8,128)S(1)} %broadcast_in_dim.2), channel_id=1, replica_groups=mesh['z'=16,'y'=4,'core'=2,'x'=4] {'z'}, dimensions={0} | all-to-all | bytes 262144 | tf_op jit(solution)/shard_map/all_to_all | solution.py:498
  78.6 8.7 %solve.1 = f32[192,2048]{1,0:T(8,128)} custom-call(f32[2,6]{1,0:T(2,128)} %bitcast.10, f32[16,16,128]{2,1,0:T(8,128)} %all_to_all.11.parts, f32[64,48]{1,0:T(8,128)} %constant.32.clone.spread, bf16[8,128,2048]{2,1,0:T(8,128)(2,1)} %get-tuple-element.21.middle_hbm, bf16[8,128,2048]{2,1,0:T(8,128)(2,1)} %get-tuple-element.22.edge_hbm), custom_call_target="tpu_custom_call" | custom-call | tf_op jit(solution)/shard_map/solve/pallas_call | solution.py:502
  (5 shorter events, 0.1 us)
Async XLA Ops:
  1.8 9.0 %collective-permute-start = (f32[16,2,8,128]{3,2,1,0:T(8,128)}, f32[16,2,8,128]{3,2,1,0:T(8,128)S(1)}, u32[]{:S(2)}, u32[]{:S(2)}) collective-permute-start(f32[16,2,8,128]{3,2,1,0:T(8,128)} %get-tuple-element.14), channel_id=1, source_target_pairs={{0,1},{1,0},{2,3},{3,2},{4,5},{5,4},{6,7},{7,6},{8,9},{9,8},{10,11... | collective-permute-start | bytes 393224 | tf_op jit(solution)/shard_map/ppermute | solution.py:428
  5.7 5.1 %collective-permute-start.1 = (f32[16,2,8,128]{3,2,1,0:T(8,128)}, f32[16,2,8,128]{3,2,1,0:T(8,128)S(1)}, u32[]{:S(2)}, u32[]{:S(2)}) collective-permute-start(f32[16,2,8,128]{3,2,1,0:T(8,128)} %get-tuple-element.15), channel_id=1, source_target_pairs={{1,2},{2,1},{5,6},{6,5},{9,10},{10,9},{13,14},{14,13},{17,18},{18,... | collective-permute-start | bytes 393224 | tf_op jit(solution)/shard_map/ppermute | solution.py:429
  10.9 16.0 %copy-start = (f32[16,2,8,128]{3,2,1,0:T(8,128)}, f32[16,2,8,128]{3,2,1,0:T(8,128)S(1)}, u32[]{:S(2)}) copy-start(f32[16,2,8,128]{3,2,1,0:T(8,128)S(1)} %broadcast_select_fusion.side) | copy-start | bytes 393220
  11.0 23.6 %collective-permute-start.3 = (f32[4,2,8,2176]{3,2,1,0:T(8,128)S(1)}, f32[4,2,8,2176]{3,2,1,0:T(8,128)S(1)}, u32[]{:S(2)}, u32[]{:S(2)}) collective-permute-start(f32[4,2,8,2176]{3,2,1,0:T(8,128)S(1)} %get-tuple-element.25), channel_id=1, source_target_pairs={{0,508},{4,8},{8,4},{12,16},{16,12},{20,24},{24,20},{28,32},{32,28... | collective-permute-start | bytes 1671176 | tf_op jit(solution)/shard_map/ppermute | solution.py:452
  15.0 19.6 %collective-permute-start.2 = (f32[4,2,8,2176]{3,2,1,0:T(8,128)S(1)}, f32[4,2,8,2176]{3,2,1,0:T(8,128)S(1)}, u32[]{:S(2)}, u32[]{:S(2)}) collective-permute-start(f32[4,2,8,2176]{3,2,1,0:T(8,128)S(1)} %get-tuple-element.26), channel_id=1, source_target_pairs={{0,4},{4,0},{1,5},{5,1},{2,6},{6,2},{3,7},{7,3},{8,12},{12,8},{9,1... | collective-permute-start | bytes 1671176 | tf_op jit(solution)/shard_map/ppermute | solution.py:455
  34.6 0.8 copy-start.1
  34.7 1.0 %copy-start.2 = (f32[4,2,8,2176]{3,2,1,0:T(8,128)}, f32[4,2,8,2176]{3,2,1,0:T(8,128)S(1)}, u32[]{:S(2)}) copy-start(f32[4,2,8,2176]{3,2,1,0:T(8,128)S(1)} %collective-permute-done.2.near) | copy-start | bytes 1671172

commit v7 on v6

--- a/solution.py
+++ b/solution.py
@@ -195,7 +195,7 @@
     whole = jnp.where(column < 32, cross, packed)
     whole = jnp.where(column < 64, whole, 0.0)
     folded = whole[0:16] + pltpu.roll(whole[16:32], 64, 1)
-    payload[...] = jnp.broadcast_to(folded[None], payload.shape)
+    payload[...] = folded
     for copy in copies:
         copy.wait()
 
@@ -478,7 +478,7 @@
         edge_kernel,
         out_shape=(
             jax.ShapeDtypeStruct((2 * HALO, 128, tile_cols), BF16),
-            jax.ShapeDtypeStruct((32, 16, LANE), F32),
+            jax.ShapeDtypeStruct((16, LANE), F32),
         ),
         in_specs=[scalar, *[vmem] * 9],
         out_specs=(far, vmem),
@@ -493,12 +493,12 @@
         name="edge",
     )(core.reshape(1), fields, side, near, across, first, second, third, partial, jnp.asarray(selection()))
 
-    parts = lax.all_to_all(payload, ("y", "core", "x"), 0, 0, tiled=True)
-    total = jnp.sum(parts, axis=0)
-    parts = lax.all_to_all(
-        jnp.broadcast_to(total[None], (lax.axis_size("z"), 16, LANE)), ("z",), 0, 0, tiled=True
-    )
-
+    for axes in (("y", "core", "x"), ("z",)):
+        copies = jnp.broadcast_to(payload[None], (lax.axis_size(axes), 16, LANE))
+        parts = lax.all_to_all(copies, axes, 0, 0, tiled=True)
+        payload = jnp.sum(parts, axis=0)
+
+    middle, edge = (pltpu.with_memory_space_constraint(x, pltpu.HBM) for x in (middle, edge))
     out = pl.pallas_call(
         solve_kernel,
         out_shape=jax.ShapeDtypeStruct((CH * tile_rows, tile_cols), F32),
@@ -510,7 +510,7 @@
             pltpu.VMEM((tile_cols // LANE, CH * tile_rows, LANE), F32),
             pltpu.SemaphoreType.DMA((2 + tile_cols // LANE,)),
         ],
-        compiler_params=params(60),
+        compiler_params=params(16),
         name="solve",
     )(shifts.T, parts, jnp.asarray(expansion()), middle, edge)
     return out.reshape(CH, tile_rows, tile_cols)

time: 88.7 us -> 88.7 us (level)
  no operation moved by 1% of the time
where the time goes in v7:
time: 88.7 us; the launch traced here: 87.5 us
  blocking collectives  34.6 us (39%)
  Pallas kernels  28.8 us (32%)
  starting transfers between devices  20.5 us (23%)
  local copies, waits for them, and re-layouts  3.03 us (3%)
    all_to_all x2, blocking collectives, per_device(): parts = lax.all_to_all(copies, axes, 0, 0, tiled=True)  34.6 us
    ppermute x1, starting transfers between devices, per_device(): lax.ppermute(jnp.where(core == 0, end, start), 'core', [(0, 1), (1, 0)])  11.8 us
    pallas_call x1, Pallas kernels, per_device(): pl.pallas_call(solve_kernel, out_shape=jax.ShapeDtypeStruct((CH * tile_ro...  8.35 us
    pallas_call x1, Pallas kernels, per_device(): pl.pallas_call(edge_kernel, out_shape=(jax.ShapeDtypeStruct((2 * HALO, 12...  7.86 us
    pallas_call x1, Pallas kernels, per_device(): pl.pallas_call(middle_kernel, out_shape=(jax.ShapeDtypeStruct((mid_rows,...  7.74 us
    ppermute x1, starting transfers between devices, per_device(): lax.ppermute(jnp.where(core == 0, start, end), gx, [(i, (i + 2 * (i % 2)...  4.05 us
    ppermute x1, starting transfers between devices, per_device(): inner = lax.ppermute(inner, 'x', [(i, i ^ 1) for i in range(gy)])  3.94 us
    pallas_call x1, Pallas kernels, per_device(): pl.pallas_call(fields_kernel, out_shape=jax.ShapeDtypeStruct(rows_of(tile...  3.04 us
  transfers between devices with their start and end apart: 4, of which 0 were waited for; matrix products, arithmetic and copies ran while one was open for 1% of the time, Pallas kernels for 12%

profile of v7, /device:TPU:1, one launch (start us, length us, event | category | flops | bytes accessed | tf_op | source)
XLA Modules:
  0.0 87.5 jit_solution(16100805675600517783)
XLA Ops:
  0.0 1.8 %edges.1 = (f32[16,2,8,128]{3,2,1,0:T(8,128)}, f32[16,2,8,128]{3,2,1,0:T(8,128)}) custom-call(s32[1]{0:T(128)} %bitcast.4.place, f32[192,2048]{1,0:T(8,128)} %bitcast.7, f32[16,2048]{1,0:T(8,128)} %diffusion.3, f32[32,2048]{1,0:T(8,128)} %bitcast.9), custom_call_target="tpu_custom_call" | custom-call | tf_op jit(solution)/shard_map/edges/pallas_call | solution.py:419
  1.8 3.9 %collective-permute-start = (f32[16,2,8,128]{3,2,1,0:T(8,128)}, f32[16,2,8,128]{3,2,1,0:T(8,128)S(1)}, u32[]{:S(2)}, u32[]{:S(2)}) collective-permute-start(f32[16,2,8,128]{3,2,1,0:T(8,128)} %get-tuple-element.14), channel_id=1, source_target_pairs={{0,1},{1,0},{2,3},{3,2},{4,5},{5,4},{6,7},{7,6},{8,9},{9,8},{10,11... | collective-permute-start | bytes 393224 | tf_op jit(solution)/shard_map/ppermute | solution.py:428
  5.8 0.7 collective-permute-start.1
  6.4 3.0 %fields.1.own = f32[16,2,8,2048]{3,2,1,0:T(8,128)} custom-call(f32[192,2048]{1,0:T(8,128)} %bitcast.8, f32[16,2048]{1,0:T(8,128)} %diffusion.3, f32[32,2048]{1,0:T(8,128)} %bitcast.10), custom_call_target="tpu_custom_call" | custom-call | flops 1000000 | bytes 4000000 | tf_op jit(solution)/shard_map/fields/pallas_call | solution.py:432
  9.5 1.3 %fusion.2 = (f32[4,2,8,2048]{3,2,1,0:T(8,128)S(1)}, f32[4,2,8,2048]{3,2,1,0:T(8,128)S(1)}) fusion(f32[16,2,8,2048]{3,2,1,0:T(8,128)} %fields.1.own), kind=kLoop, calls=%fused_computation.6 | loop fusion | bytes 2097152 | tf_op jit(solution)/shard_map/slice | solution.py:449
  10.8 0.0 collective-permute-done
  10.8 0.0 collective-permute-done.1
  10.8 0.0 copy-start.2
  10.9 0.1 fusion
  10.9 4.0 %collective-permute-start.3 = (f32[4,2,8,2176]{3,2,1,0:T(8,128)S(1)}, f32[4,2,8,2176]{3,2,1,0:T(8,128)S(1)}, u32[]{:S(2)}, u32[]{:S(2)}) collective-permute-start(f32[4,2,8,2176]{3,2,1,0:T(8,128)S(1)} %get-tuple-element.25), channel_id=1, source_target_pairs={{0,508},{4,8},{8,4},{12,16},{16,12},{20,24},{24,20},{28,32},{32,28... | collective-permute-start | bytes 1671176 | tf_op jit(solution)/shard_map/ppermute | solution.py:452
  15.0 11.8 %collective-permute-start.2 = (f32[4,2,8,2176]{3,2,1,0:T(8,128)S(1)}, f32[4,2,8,2176]{3,2,1,0:T(8,128)S(1)}, u32[]{:S(2)}, u32[]{:S(2)}) collective-permute-start(f32[4,2,8,2176]{3,2,1,0:T(8,128)S(1)} %get-tuple-element.26), channel_id=1, source_target_pairs={{0,4},{4,0},{1,5},{5,1},{2,6},{6,2},{3,7},{7,3},{8,12},{12,8},{9,1... | collective-permute-start | bytes 1671176 | tf_op jit(solution)/shard_map/ppermute | solution.py:455
  26.8 0.0 copy-done.2
  26.9 7.7 %middle.1 = (bf16[8,128,2048]{2,1,0:T(8,128)(2,1)}, f32[6,2,8,2176]{3,2,1,0:T(8,128)}, f32[4,2,8,2176]{3,2,1,0:T(8,128)}, f32[4,2,8,2176]{3,2,1,0:T(8,128)}, f32[160,160]{1,0:T(8,128)}) custom-call(f32[16,2,8,2048]{3,2,1,0:T(8,128)} %fields.1.own, f32[16,2,8,128]{3,2,1,0:T(8,128)} %copy-done.2), custom_call_target="tpu_custom_call" | custom-call | flops 1000000000 | bytes 20000000 | tf_op jit(solution)/shard_map/middle/pallas_call | solution.py:456
  34.6 0.0 collective-permute-done.3.across
  34.6 0.0 copy-start.3
  34.6 0.0 collective-permute-done.2.near
  34.6 0.0 copy-start.4
  34.6 0.8 copy-done.3
  35.4 0.2 copy-done.4
  35.7 0.0 copy-start
  35.7 0.0 copy-start.1
  35.7 7.9 %edge.1 = (bf16[8,128,2048]{2,1,0:T(8,128)(2,1)}, f32[16,128]{1,0:T(8,128)}) custom-call(s32[1]{0:T(128)} %bitcast.1.core, f32[16,2,8,2048]{3,2,1,0:T(8,128)} %fields.1.own, f32[16,2,8,128]{3,2,1,0:T(8,128)} %copy-done.2, f32[4,2,8,2176]{3,2,1,0:T(8,128)} %copy-done.4, f32[4,2,8,2176]{3,2,1,0:T(8,128)} %copy-done.3, ...), custom_call_target="tpu_custom_call" | custom-call | tf_op jit(solution)/shard_map/edge/pallas_call | solution.py:477
  43.5 0.7 broadcast_in_dim.4
  44.3 14.2 %all_to_all.10 = f32[32,16,128]{2,1,0:T(8,128)S(1)} all-to-all(f32[32,16,128]{2,1,0:T(8,128)S(1)} %broadcast_in_dim.4), channel_id=1, replica_groups=mesh['z'=16,'y'=4,'core'=2,'x'=4] {'y','core','x'}, dimensions={0} | all-to-all | bytes 524288 | tf_op jit(solution)/shard_map/all_to_all | solution.py:498
  58.5 20.4 %all_to_all.11.parts = f32[16,16,128]{2,1,0:T(8,128)S(1)} all-to-all(f32[16,16,128]{2,1,0:T(8,128)S(1)} %broadcast_in_dim.5), channel_id=1, replica_groups=mesh['z'=16,'y'=4,'core'=2,'x'=4] {'z'}, dimensions={0} | all-to-all | bytes 262144 | tf_op jit(solution)/shard_map/all_to_all | solution.py:498
  78.9 0.0 copy-done
  78.9 0.0 copy-done.1
  78.9 8.3 %solve.1 = f32[192,2048]{1,0:T(8,128)} custom-call(f32[2,6]{1,0:T(2,128)S(1)} %bitcast.6, f32[16,16,128]{2,1,0:T(8,128)S(1)} %all_to_all.11.parts, f32[64,48]{1,0:T(8,128)S(1)} %copy-done, bf16[8,128,2048]{2,1,0:T(8,128)(2,1)} %get-tuple-element.21.middle_hbm, bf16[8,128,2048]{2,1,0:T(8,128)(2,1)} %get-tuple-element.22.edge_hbm), custom_call_target="tpu_custom_call" | custom-call | tf_op jit(solution)/shard_map/solve/pallas_call | solution.py:502
  (5 shorter events, 0.1 us)
Async XLA Ops:
  1.8 9.0 %collective-permute-start = (f32[16,2,8,128]{3,2,1,0:T(8,128)}, f32[16,2,8,128]{3,2,1,0:T(8,128)S(1)}, u32[]{:S(2)}, u32[]{:S(2)}) collective-permute-start(f32[16,2,8,128]{3,2,1,0:T(8,128)} %get-tuple-element.14), channel_id=1, source_target_pairs={{0,1},{1,0},{2,3},{3,2},{4,5},{5,4},{6,7},{7,6},{8,9},{9,8},{10,11... | collective-permute-start | bytes 393224 | tf_op jit(solution)/shard_map/ppermute | solution.py:428
  5.8 5.0 %collective-permute-start.1 = (f32[16,2,8,128]{3,2,1,0:T(8,128)}, f32[16,2,8,128]{3,2,1,0:T(8,128)S(1)}, u32[]{:S(2)}, u32[]{:S(2)}) collective-permute-start(f32[16,2,8,128]{3,2,1,0:T(8,128)} %get-tuple-element.15), channel_id=1, source_target_pairs={{1,2},{2,1},{5,6},{6,5},{9,10},{10,9},{13,14},{14,13},{17,18},{18,... | collective-permute-start | bytes 393224 | tf_op jit(solution)/shard_map/ppermute | solution.py:429
  10.8 16.0 %copy-start.2 = (f32[16,2,8,128]{3,2,1,0:T(8,128)}, f32[16,2,8,128]{3,2,1,0:T(8,128)S(1)}, u32[]{:S(2)}) copy-start(f32[16,2,8,128]{3,2,1,0:T(8,128)S(1)} %broadcast_select_fusion.side) | copy-start | bytes 393220
  10.9 23.7 %collective-permute-start.3 = (f32[4,2,8,2176]{3,2,1,0:T(8,128)S(1)}, f32[4,2,8,2176]{3,2,1,0:T(8,128)S(1)}, u32[]{:S(2)}, u32[]{:S(2)}) collective-permute-start(f32[4,2,8,2176]{3,2,1,0:T(8,128)S(1)} %get-tuple-element.25), channel_id=1, source_target_pairs={{0,508},{4,8},{8,4},{12,16},{16,12},{20,24},{24,20},{28,32},{32,28... | collective-permute-start | bytes 1671176 | tf_op jit(solution)/shard_map/ppermute | solution.py:452
  15.0 19.6 %collective-permute-start.2 = (f32[4,2,8,2176]{3,2,1,0:T(8,128)S(1)}, f32[4,2,8,2176]{3,2,1,0:T(8,128)S(1)}, u32[]{:S(2)}, u32[]{:S(2)}) collective-permute-start(f32[4,2,8,2176]{3,2,1,0:T(8,128)S(1)} %get-tuple-element.26), channel_id=1, source_target_pairs={{0,4},{4,0},{1,5},{5,1},{2,6},{6,2},{3,7},{7,3},{8,12},{12,8},{9,1... | collective-permute-start | bytes 1671176 | tf_op jit(solution)/shard_map/ppermute | solution.py:455
  34.6 0.8 copy-start.3
  34.6 1.0 %copy-start.4 = (f32[4,2,8,2176]{3,2,1,0:T(8,128)}, f32[4,2,8,2176]{3,2,1,0:T(8,128)S(1)}, u32[]{:S(2)}) copy-start(f32[4,2,8,2176]{3,2,1,0:T(8,128)S(1)} %collective-permute-done.2.near) | copy-start | bytes 1671172
  35.7 43.3 %copy-start = (f32[64,48]{1,0:T(8,128)S(1)}, f32[64,48]{1,0:T(8,128)}, u32[]{:S(2)}) copy-start(f32[64,48]{1,0:T(8,128)} %constant.32.clone.spread) | copy-start | bytes 36868
  35.7 43.3 %copy-start.1 = (f32[6,2]{0,1:T(2,128)S(1)}, f32[6,2]{0,1:T(2,128)}, u32[]{:S(2)}) copy-start(f32[6,2]{0,1:T(2,128)} %param.9) | copy-start | bytes 148
